TPU v7x, 256 devices: a whole 4x4x8 slice. The times are simulated.
256 devices in a mesh: tm: 4 (over x), rows: 32 (over z, y), clip: 2 (over core).
Axes of the slice: x: 4, y: 4, z: 8, core: 2. Of those that a mesh axis runs over, the one named last changes fastest.
Arguments:
- features: bfloat16 [8, 16, 64, 9984], P('clip', 'tm', 'rows'), may hold values from -6 to 6
- lengths: int32 [8], replicated, may hold values from 1 to 16, as said below
- stored_slot: int32 [8], replicated, may hold values from 0 to 7, each once
- owner_slot: int32 [8], replicated, may hold values from 0 to 7, each once
- gain_first: float32 [96], replicated, may hold values from 0.1 to 1.9
- conv_first: bfloat16 [3, 3, 3, 96, 96], replicated, may hold values from -0.125 to 0.125
- bias_first: float32 [96], replicated, may hold values from -3 to 3
- gain_second: float32 [96], replicated, may hold values from 0.1 to 1.9
- conv_second: bfloat16 [3, 3, 3, 96, 96], replicated, may hold values from -0.125 to 0.125
- bias_second: float32 [96], replicated, may hold values from -3 to 3
- reduce_conv_weight: bfloat16 [3, 3, 96, 96], replicated, may hold values from -0.21875 to 0.21875
- reduce_conv_bias: float32 [96], replicated, may hold values from -3 to 3
Outputs:
- encoded: bfloat16 [8, 16, 32, 4992], P('clip', 'tm', 'rows')
Inputs may be any that keep to these rules, and one draw needn't show every extreme that they name: `lengths`: some clip has all 16 frames. `stored_slot`: each clip has its own storage slot. `owner_slot`: each clip has its own output slot.
All inputs are finite; a program needn't handle non-finite values.
Results may differ from a plain program's by a relative error of at most 0.0051.
Values may be sent and summed in bfloat16 or wider, within the bound.
A program may use at most 64 MiB of HBM per device.

v0:
```python
import jax
import jax.numpy as jnp
from jax import lax
from jax.experimental import pallas as pl
from jax.experimental.pallas import tpu as pltpu
from jax.sharding import PartitionSpec as P

NORM_EPS = 1e-06
MESH = pl.DeviceIdType.MESH
F32 = jnp.float32
BF16 = jnp.bfloat16

CH = 96
XB = 4
YB = 4
ZB = 8
OWN = 26
GROUPS = 9
WIN = GROUPS * 4
PADL = 384
PADR = 768
LANES = 128
PAIRS1 = 15
PAIRS2 = 14
BC = 2 * PAIRS1
OC = 2 * PAIRS2
JC = 13


def lane_iota(shape):
    return lax.broadcasted_iota(jnp.int32, shape, len(shape) - 1)


def shifted(flat, step, frame):
    return jnp.where(frame < step, 0.0, pltpu.roll(flat, step, 0))


def silu(u):
    return 0.5 * u * (1.0 + jnp.tanh(0.5 * u))


def norm_act(v, gain):
    mean = jnp.sum(v * v, axis=-1, keepdims=True) * (1.0 / CH)
    return silu(v * lax.rsqrt(mean + NORM_EPS) * gain)


def build_toeplitz(w_ref, wt):
    wt[...] = jnp.zeros_like(wt)

    def tap(i, _):
        for n in range(2):
            for k in range(3):
                wt[i, pl.ds(128 * (n + k), CH), pl.ds(128 * n, CH)] = w_ref[3 * i + k]
        return 0

    lax.fori_loop(0, 9, tap, 0)


def conv_lhs(src, base, p0, pairs, rows):
    parts = []
    for t in range(3):
        for j in range(3):
            for k in range(4):
                pieces = [
                    src[t, base + 2 * (p0 + p) + k, j : j + rows].reshape(rows * 16, LANES)
                    for p in range(pairs)
                ]
                parts.append(jnp.concatenate(pieces, axis=0))
    return jnp.concatenate(parts, axis=1)


def kernel(
    feat, w1, w2, wr, g1, b1, g2, b2, br, lengths, stored, owner, out,
    arr, xs, a, b, wt1, wt2, rw, ob, sb, gb, ha, hb, ho,
    s_a, r_a, s_z, r_z, s_g, r_g, s_c, r_c, l_sem,
):
    x = lax.axis_index("tm")
    zy = lax.axis_index("rows")
    core = lax.axis_index("clip")
    z, y = zy // YB, zy % YB
    me = x * YB + y
    up = ((z + ZB - 1) % ZB) * YB + y
    down = ((z + 1) % ZB) * YB + y

    def plane(i):
        t = (me + i) % 16
        return t, (t // YB, z * YB + t % YB, core)

    def start_lane(q):
        return pl.multiple_of(PADL + CH * (OWN * q - 4 + 2 * (q % 2)), 128)

    barrier = pltpu.get_barrier_semaphore()

    def greet(i, _):
        _, dev = plane(i)
        pl.semaphore_signal(barrier, inc=1, device_id=dev, device_id_type=MESH)
        return 0

    lax.fori_loop(1, 16, greet, 0)
    for dev in ((x, up, core), (x, down, core), (x, zy, 1 - core)):
        pl.semaphore_signal(barrier, inc=1, device_id=dev, device_id_type=MESH)
    pl.semaphore_wait(barrier, 18)

    def send_in(i):
        t, dev = plane(i)
        return pltpu.make_async_remote_copy(
            src_ref=feat.at[t // YB, :, pl.ds(start_lane(t % YB), WIN * CH)],
            dst_ref=arr.at[me],
            send_sem=s_a.at[t],
            recv_sem=r_a.at[me],
            device_id=dev,
            device_id_type=MESH,
        )

    def start_in(i, _):
        send_in(i).start()
        return 0

    lax.fori_loop(1, 16, start_in, 0)
    own_in = pltpu.make_async_copy(
        feat.at[x, :, pl.ds(start_lane(y), WIN * CH)], arr.at[me], l_sem
    )
    own_in.start()

    build_toeplitz(w1, wt1)
    build_toeplitz(w2, wt2)
    rw[...] = jnp.zeros_like(rw)

    def tap(i, _):
        rw[pl.ds(pl.multiple_of(128 * i, 128), CH), pl.ds(0, CH)] = wr[i]
        return 0

    lax.fori_loop(0, 9, tap, 0)

    own_in.wait()

    def wait_in(i, _):
        t, dev = plane(i)
        pltpu.make_async_remote_copy(
            src_ref=feat.at[0, :, pl.ds(0, WIN * CH)],
            dst_ref=arr.at[t],
            send_sem=s_a.at[t],
            recv_sem=r_a.at[t],
            device_id=dev,
            device_id_type=MESH,
        ).wait_recv()
        return 0

    lax.fori_loop(1, 16, wait_in, 0)

    gain1 = g1[...]
    gain2 = g2[...]
    lane8 = lane_iota((XB, 8, LANES))
    sub8 = lax.broadcasted_iota(jnp.int32, (8, LANES), 0)
    frame128 = lax.broadcasted_iota(jnp.int32, (128, LANES), 0) % 16

    def act_step(i, _):
        q, g = i // GROUPS, i % GROUPS
        lane0 = pl.multiple_of(g * 384, 128)
        v = [
            jnp.stack([arr[XB * xb + q, :, pl.ds(lane0 + 128 * m, 128)].astype(F32) for xb in range(XB)])
            for m in range(3)
        ]

        def rl(u, s):
            return pltpu.roll(u.reshape(XB * 8, LANES), s, 1).reshape(XB, 8, LANES)

        cols = [
            jnp.where(lane8 < 96, v[0], 0.0),
            jnp.where(lane8 < 32, rl(v[0], 32), jnp.where(lane8 < 96, rl(v[1], 32), 0.0)),
            jnp.where(lane8 < 64, rl(v[1], 64), jnp.where(lane8 < 96, rl(v[2], 64), 0.0)),
            jnp.where(lane8 < 96, rl(v[2], 96), 0.0),
        ]
        tiles = []
        for c in cols:
            turned = [pltpu.roll(c[xb], 4, 0) for xb in range(XB)]
            tiles += [jnp.where(sub8 < 4, c[0], turned[1]), jnp.where(sub8 < 4, c[2], turned[3])]
            tiles += [jnp.where(sub8 < 4, turned[0], c[1]), jnp.where(sub8 < 4, turned[2], c[3])]
        flat = jnp.concatenate(tiles, axis=0)
        w0 = 4 * g
        row = 2 * q
        xs[pl.ds(w0, 4), pl.ds(row, 2)] = flat.astype(BF16).reshape(4, 2, 16, LANES)
        act = norm_act(flat, gain1)
        for t in range(3):
            moved = act if t == 2 else shifted(act, 2 - t, frame128)
            a[t, pl.ds(w0, 4), pl.ds(row + 1, 2)] = moved.astype(BF16).reshape(4, 2, 16, LANES)
        return 0

    lax.fori_loop(0, YB * GROUPS, act_step, 0)

    def exchange(src_first, src_last, halo, k):
        copies = []
        if src_first is not None:
            copies.append(
                pltpu.make_async_remote_copy(
                    src_ref=src_first, dst_ref=halo.at[1], send_sem=s_z.at[k], recv_sem=r_z.at[k],
                    device_id=(x, up, core), device_id_type=MESH,
                )
            )
        if src_last is not None:
            copies.append(
                pltpu.make_async_remote_copy(
                    src_ref=src_last, dst_ref=halo.at[0], send_sem=s_z.at[k + 1], recv_sem=r_z.at[k + 1],
                    device_id=(x, down, core), device_id_type=MESH,
                )
            )
        for c in copies:
            c.start()
        return copies

    inside = (z > 0, z < ZB - 1)
    frame32 = lax.broadcasted_iota(jnp.int32, (32, LANES), 0) % 16

    def fill_halo(halo, dst, cols):
        def step(i, _):
            for side in range(2):
                v = halo[side, pl.ds(2 * i, 2)].astype(F32).reshape(32, LANES)
                v = jnp.where(inside[side], v, 0.0)
                for t in range(3):
                    moved = v if t == 2 else shifted(v, 2 - t, frame32)
                    dst[t, pl.ds(2 * i, 2), 9 * side] = moved.astype(BF16).reshape(2, 16, LANES)
            return 0

        lax.fori_loop(0, cols // 2, step, 0)

    copies = exchange(a.at[2, :, 1], a.at[2, :, 8], ha, 0)
    for c in copies:
        c.wait()
    fill_halo(ha, a, WIN)

    base = 2 * (1 - y % 2)
    col0 = OWN * y

    P1 = 3
    bias1 = b1[...]
    bias2 = b2[...]

    def conv1_step(i, _):
        acc = jnp.dot(conv_lhs(a, base, P1 * i, P1, 8), wt1[...].reshape(4608, 256), preferred_element_type=F32)
        for p in range(P1):
            for n in range(2):
                bcol = 2 * (P1 * i + p) + n
                v = acc[128 * p : 128 * p + 128, 128 * n : 128 * n + 128] + bias1
                act = norm_act(v, gain2)
                image = col0 - 1 + bcol
                act = jnp.where(jnp.logical_and(image >= 0, image < 104), act, 0.0)
                for t in range(3):
                    moved = act if t == 2 else shifted(act, 2 - t, frame128)
                    b[t, bcol, 1:9] = moved.astype(BF16).reshape(8, 16, LANES)
        return 0

    lax.fori_loop(0, PAIRS1 // P1, conv1_step, 0)

    copies = exchange(b.at[2, :, 1], b.at[2, :, 8], hb, 2)
    for c in copies:
        c.wait()
    fill_halo(hb, b, BC)

    P2 = 2

    def conv2_step(i, _):
        acc = jnp.dot(conv_lhs(b, 0, P2 * i, P2, 8), wt2[...].reshape(4608, 256), preferred_element_type=F32)
        for p in range(P2):
            for n in range(2):
                c = 2 * (P2 * i + p) + n
                v = acc[128 * p : 128 * p + 128, 128 * n : 128 * n + 128] + bias2
                v = v + xs[base + 2 + c].reshape(128, LANES).astype(F32)
                v = jnp.where(col0 + c < 104, v, 0.0)
                ob[c, 0:8] = v.astype(BF16).reshape(8, 16, LANES)
        return 0

    lax.fori_loop(0, PAIRS2 // P2, conv2_step, 0)

    copies = exchange(ob.at[:, 0], None, ho, 4)
    for c in copies:
        c.wait()

    def fill_last(c, _):
        ob[c, 8] = jnp.where(z < ZB - 1, ho[1, c].astype(F32), 0.0).astype(BF16)
        return 0

    lax.fori_loop(0, OC, fill_last, 0)

    bias_r = br[...]

    def reduce_step(jj, _):
        pieces = []
        for j2 in range(3):
            for k in range(3):
                rows = []
                for n in range(2):
                    c = jnp.minimum(4 * jj + 2 * n + k, OC - 1)
                    rows += [ob[c, 2 * i + j2] for i in range(4)]
                pieces.append(jnp.concatenate(rows, axis=0))
        acc = jnp.dot(jnp.concatenate(pieces, axis=1), rw[...], preferred_element_type=F32) + bias_r
        for i in range(4):
            for h in range(2):
                e = acc[16 * i + 8 * h : 16 * i + 8 * h + 8]
                o = acc[64 + 16 * i + 8 * h : 64 + 16 * i + 8 * h + 8]
                sb[2 * h, i, jj] = jnp.where(sub8 < 4, e, pltpu.roll(o, 4, 0)).astype(BF16)
                sb[2 * h + 1, i, jj] = jnp.where(sub8 < 4, pltpu.roll(e, 4, 0), o).astype(BF16)
        return 0

    lax.fori_loop(0, 7, reduce_step, 0)

    slot = XB * core + x

    def send_out(i):
        t, dev = plane(i)
        return pltpu.make_async_remote_copy(
            src_ref=sb.at[t // YB, t % YB],
            dst_ref=gb.at[slot, y],
            send_sem=s_g.at[t],
            recv_sem=r_g.at[me],
            device_id=dev,
            device_id_type=MESH,
        )

    def start_out(i, _):
        send_out(i).start()
        return 0

    lax.fori_loop(1, 16, start_out, 0)
    own_out = pltpu.make_async_copy(sb.at[x, y], gb.at[slot, y], l_sem)
    own_out.start()
    own_out.wait()

    def wait_out(i, _):
        t, dev = plane(i)
        pltpu.make_async_remote_copy(
            src_ref=sb.at[0, 0],
            dst_ref=gb.at[XB * core + t // YB, t % YB],
            send_sem=s_g.at[t],
            recv_sem=r_g.at[t],
            device_id=dev,
            device_id_type=MESH,
        ).wait_recv()
        return 0

    lax.fori_loop(1, 16, wait_out, 0)

    swap = pltpu.make_async_remote_copy(
        src_ref=gb.at[pl.ds(XB * core, XB)],
        dst_ref=gb.at[pl.ds(XB * core, XB)],
        send_sem=s_c,
        recv_sem=r_c,
        device_id=(x, zy, 1 - core),
        device_id_type=MESH,
    )
    swap.start()
    swap.wait()

    lane4 = lane_iota((8, LANES))
    for s in range(XB):
        src = jnp.int32(0)
        length = jnp.int32(0)
        for c in range(8):
            hit = owner[c] == XB * core + s
            src = jnp.where(hit, stored[c], src)
            length = jnp.where(hit, lengths[c], length)
        alive = (XB * x + sub8 % 4) < length

        for q in range(YB):
            tiles = gb[src, q]
            if q == 0:
                columns = []
            for j in range(JC):
                tile = tiles[j // 2].astype(F32)
                columns.append(tile if j % 2 == 0 else pltpu.roll(tile, 4, 0))
        for g in range(13):
            c0, c1, c2, c3 = columns[4 * g : 4 * g + 4]
            t1, t2, t3 = pltpu.roll(c1, 96, 1), pltpu.roll(c2, 64, 1), pltpu.roll(c3, 32, 1)
            dense = [jnp.where(lane4 < 96, c0, t1), jnp.where(lane4 < 64, t1, t2), jnp.where(lane4 < 32, t2, t3)]
            for m in range(3):
                out[s, :, pl.ds(384 * g + 128 * m, 128)] = jnp.where(alive, dense[m], 0.0)[0:4].astype(BF16)

    def end_sends(i, _):
        send_in(i).wait_send()
        send_out(i).wait_send()
        return 0

    lax.fori_loop(1, 16, end_sends, 0)


def local(
    features, lengths, stored_slot, owner_slot, gain_first, conv_first, bias_first,
    gain_second, conv_second, bias_second, reduce_conv_weight, reduce_conv_bias,
):
    slots, frames, rows, lanes = features.shape
    feat = jnp.transpose(features, (0, 2, 1, 3)).reshape(slots, rows * frames, lanes)
    feat = jnp.pad(feat, ((0, 0), (0, 0), (PADL, PADR)))

    def vec(v):
        return jnp.pad(v, (0, LANES - CH)).reshape(1, LANES)

    vmem = pl.BlockSpec(memory_space=pltpu.VMEM)
    smem = pl.BlockSpec(memory_space=pltpu.SMEM)
    result = pl.pallas_call(
        kernel,
        out_shape=jax.ShapeDtypeStruct((slots, frames, 4992), BF16),
        in_specs=[pl.BlockSpec(memory_space=pl.ANY)] + [vmem] * 8 + [smem] * 3,
        out_specs=vmem,
        scratch_shapes=[
            pltpu.VMEM((16, 8, WIN * CH), BF16),
            pltpu.VMEM((WIN, 8, 16, LANES), BF16),
            pltpu.VMEM((3, WIN, 10, 16, LANES), BF16),
            pltpu.VMEM((3, BC, 10, 16, LANES), BF16),
            pltpu.VMEM((9, 512, 256), BF16),
            pltpu.VMEM((9, 512, 256), BF16),
            pltpu.VMEM((1152, 128), BF16),
            pltpu.VMEM((OC, 9, 16, LANES), BF16),
            pltpu.VMEM((XB, 4, 7, 8, LANES), BF16),
            pltpu.VMEM((2 * XB, YB, 7, 8, LANES), BF16),
            pltpu.VMEM((2, WIN, 16, LANES), BF16),
            pltpu.VMEM((2, BC, 16, LANES), BF16),
            pltpu.VMEM((2, OC, 16, LANES), BF16),
            pltpu.SemaphoreType.DMA((16,)),
            pltpu.SemaphoreType.DMA((16,)),
            pltpu.SemaphoreType.DMA((6,)),
            pltpu.SemaphoreType.DMA((6,)),
            pltpu.SemaphoreType.DMA((16,)),
            pltpu.SemaphoreType.DMA((16,)),
            pltpu.SemaphoreType.DMA,
            pltpu.SemaphoreType.DMA,
            pltpu.SemaphoreType.DMA,
        ],
        compiler_params=pltpu.CompilerParams(
            collective_id=0, has_side_effects=True, vmem_limit_bytes=50 << 20
        ),
        name="encode",
    )(
        feat,
        conv_first.reshape(27, CH, CH),
        conv_second.reshape(27, CH, CH),
        reduce_conv_weight.reshape(9, CH, CH),
        vec(gain_first), vec(bias_first), vec(gain_second), vec(bias_second), vec(reduce_conv_bias),
        lengths, stored_slot, owner_slot,
    )
    return result.reshape(slots, frames, 1, 4992)


def solution(mesh):
    spec = P("clip", "tm", "rows", None)
    return jax.shard_map(
        local, mesh=mesh, in_specs=(spec,) + (P(),) * 11, out_specs=spec, check_vma=False
    )
```

profile of v0, /device:TPU:1, one launch (start us, length us, event | category | flops | bytes accessed | tf_op | source)
XLA Modules:
  0.0 72.7 jit_solution(13195098215714520695)
XLA Ops:
  0.0 1.3 %copy.13 = bf16[4,2,4,9984]{3,2,1,0:T(4,128)(2,1)S(1)} copy(bf16[4,2,4,9984]{3,1,2,0:T(2,128)(2,1)} %bitcast.21) | data formatting | bytes 1277952 | tf_op jit(solution)/shard_map/transpose | solution.py:390
  1.3 0.0 copy-start.2
  1.3 0.1 reshape.30
  1.5 0.0 copy-start
  1.5 0.0 copy-start.1
  1.5 0.1 pad.20.feat
  1.6 0.0 copy-start.10
  1.6 0.7 %copy-done.10 = f32[96]{0:T(128)S(1)} copy-done((f32[96]{0:T(128)S(1)}, f32[96]{0:T(128)}, u32[]{:S(2)}) %copy-start.10) | copy-done | bytes 408
  2.3 0.0 copy-start.6
  2.3 0.0 copy-start.7
  2.3 0.6 copy-done.6
  3.0 0.0 copy-done.7
  3.0 0.0 copy-start.8
  3.0 0.0 copy-start.9
  3.0 0.7 copy-done.8
  3.7 0.0 copy-done.9
  3.7 0.0 copy-start.3
  3.7 0.0 copy-start.4
  3.7 0.0 copy-start.5
  3.7 0.0 copy-done.2
  3.7 0.0 copy-done
  3.7 0.0 copy-done.1
  3.7 0.6 copy-done.3
  4.3 0.0 copy-done.4
  4.3 0.0 copy-done.5
  4.4 67.7 %encode.1 = bf16[4,4,4992]{2,1,0:T(4,128)(2,1)S(1)} custom-call(bf16[4,8,11136]{2,1,0:T(8,128)(2,1)S(1)} %pad.20.feat, bf16[27,96,96]{2,1,0:T(8,128)(2,1)S(1)} %bitcast.17, bf16[27,96,96]{2,1,0:T(8,128)(2,1)S(1)} %bitcast.18, bf16[9,96,96]{2,1,0:T(8,128)(2,1)S(1)} %bitcast.20, f32[1,128]{1,0:T(1,128)S(1)} %pad_bitcast_fusion.4.g1, ...), custom_call_target="tpu_custom_call" | custom-call | tf_op jit(solution)/shard_map/encode/pallas_call | solution.py:398
  72.0 0.7 copy.16
  (3 shorter events, 0.0 us)
Async XLA Ops:
  1.3 2.4 %copy-start.2 = (bf16[3,3,96,96]{3,2,1,0:T(8,128)(2,1)S(1)}, bf16[3,3,96,96]{3,2,1,0:T(8,128)(2,1)}, u32[]{:S(2)}) copy-start(bf16[3,3,96,96]{3,2,1,0:T(8,128)(2,1)} %param.22) | copy-start | bytes 497668
  1.5 2.2 %copy-start = (bf16[3,3,3,96,96]{4,3,2,1,0:T(8,128)(2,1)S(1)}, bf16[3,3,3,96,96]{4,3,2,1,0:T(8,128)(2,1)}, u32[]{:S(2)}) copy-start(bf16[3,3,3,96,96]{4,3,2,1,0:T(8,128)(2,1)} %param.17) | copy-start | bytes 1492996
  1.5 2.2 %copy-start.1 = (bf16[3,3,3,96,96]{4,3,2,1,0:T(8,128)(2,1)S(1)}, bf16[3,3,3,96,96]{4,3,2,1,0:T(8,128)(2,1)}, u32[]{:S(2)}) copy-start(bf16[3,3,3,96,96]{4,3,2,1,0:T(8,128)(2,1)} %param.20) | copy-start | bytes 1492996
  1.6 0.7 %copy-start.10 = (f32[96]{0:T(128)S(1)}, f32[96]{0:T(128)}, u32[]{:S(2)}) copy-start(f32[96]{0:T(128)} %param.16) | copy-start | bytes 1156
  2.3 0.7 copy-start.6
  2.3 0.7 copy-start.7
  3.0 0.7 copy-start.8
  3.0 0.7 copy-start.9
  3.7 0.7 copy-start.3
  3.7 0.7 copy-start.4
  3.7 0.7 copy-start.5
where the time goes:
time: 72.9 us; the launch traced here: 72.7 us
  Pallas kernels  67.7 us (93%)
  local copies, waits for them, and re-layouts  4.94 us (7%)
    pallas_call x1, Pallas kernels, local(): pl.pallas_call(kernel, out_shape=jax.ShapeDtypeStruct((slots, frames, 499...  67.7 us
    unnamed x23, local copies, waits for them, and re-layouts  3.41 us

commit v1 on v0

v1 whole, which is shorter than its diff:
```python
import jax
import jax.numpy as jnp
from jax import lax
from jax.experimental import pallas as pl
from jax.experimental.pallas import tpu as pltpu
from jax.sharding import PartitionSpec as P

NORM_EPS = 1e-06
MESH = pl.DeviceIdType.MESH
F32 = jnp.float32
BF16 = jnp.bfloat16

CH = 96
XB = 4
YB = 4
ZB = 8
OWN = 26
GROUPS = 9
WIN = GROUPS * 4
PADL = 384
PADR = 768
LANES = 128
PAIRS1 = 15
PAIRS2 = 14
BC = 2 * PAIRS1
OC = 2 * PAIRS2
JC = 13


def shifted(flat, step, frame):
    return jnp.where(frame < step, 0.0, pltpu.roll(flat, step, 0))


def silu(u):
    return 0.5 * u * (1.0 + jnp.tanh(0.5 * u))


def split_square(v):
    sq = v * v
    hi = sq.astype(BF16)
    return hi, (sq - hi.astype(F32)).astype(BF16)


def scaled_act(v, total, gain):
    return silu(v * lax.rsqrt(total * (1.0 / CH) + NORM_EPS) * gain)


def build_toeplitz(w_ref, wt):
    def tap(i, _):
        for n in range(2):
            for k in range(3):
                wt[i, pl.ds(128 * (n + k), CH), pl.ds(128 * n, CH)] = w_ref[3 * i + k]
        return 0

    lax.fori_loop(0, 9, tap, 0)


def conv_lhs(src, col0, pairs, rows):
    parts = []
    for t in range(3):
        for j in range(3):
            for k in range(4):
                pieces = []
                for p in range(pairs):
                    for first, count in rows:
                        block = src[t, col0 + 2 * p + k, first + j : first + j + count]
                        pieces.append(block.reshape(count * 16, LANES))
                parts.append(jnp.concatenate(pieces, axis=0))
    return jnp.concatenate(parts, axis=1)


INNER = ((1, 6),)
EDGES = ((0, 1), (7, 1))


def kernel(
    feat, w1h, w2h, wrh, g1h, b1h, g2h, b2h, brh, lenh, stoh, ownh, out,
    arr, xs, a, b, wt1, wt2, rw, ob, sb, gb, ha, hb, ho, w1, w2, wr, vin, vec, ones2,
    lengths, stored, owner,
    s_a, r_a, s_z, r_z, s_g, r_g, l_a, l_w,
):
    x = lax.axis_index("tm")
    zy = lax.axis_index("rows")
    core = lax.axis_index("clip")
    z, y = zy // YB, zy % YB
    me = x * YB + y
    up = ((z + ZB - 1) % ZB) * YB + y
    down = ((z + 1) % ZB) * YB + y

    def plane(i):
        t = (me + i) % 16
        return t, (t // YB, z * YB + t % YB, core)

    def start_lane(q):
        return pl.multiple_of(PADL + CH * (OWN * q - 4 + 2 * (q % 2)), 128)

    arr[:, :, 0:128] = jnp.zeros((16, 8, 128), BF16)
    arr[:, :, 3072:3456] = jnp.zeros((16, 8, 384), BF16)
    barrier = pltpu.get_barrier_semaphore()

    def greet(i, _):
        t = (me + i) % 16
        c = (core + i // 16) % 2
        pl.semaphore_signal(
            barrier, inc=1, device_id=(t // YB, z * YB + t % YB, c), device_id_type=MESH
        )
        return 0

    lax.fori_loop(1, 32, greet, 0)
    for row in (up, down):
        pl.semaphore_signal(barrier, inc=1, device_id=(x, row, core), device_id_type=MESH)

    loads = [
        pltpu.make_async_copy(src, dst, l_w.at[i])
        for i, (src, dst) in enumerate(
            [(w1h, w1), (w2h, w2), (wrh, wr)]
            + [(v, vin.at[i]) for i, v in enumerate((g1h, b1h, g2h, b2h, brh))]
            + [(lenh, lengths), (stoh, stored), (ownh, owner)]
        )
    ]
    for c in loads:
        c.start()

    def zero_weights(i, _):
        wt1[i] = jnp.zeros((512, 256), BF16)
        wt2[i] = jnp.zeros((512, 256), BF16)
        return 0

    lax.fori_loop(0, 9, zero_weights, 0)
    rw[...] = jnp.zeros_like(rw)
    vec[...] = jnp.zeros_like(vec)
    r_i = lax.broadcasted_iota(jnp.int32, (256, 256), 0) // 128
    c_i = lax.broadcasted_iota(jnp.int32, (256, 256), 1) // 128
    ones2[...] = jnp.where(r_i == c_i, 1.0, 0.0).astype(BF16)
    loads[0].wait()
    build_toeplitz(w1, wt1)
    pl.semaphore_wait(barrier, 33)

    HALF = 1536
    odd = y % 2

    def in_copy(i, chunk):
        t, dev = plane(i)
        q = t % YB
        off = 128 * (1 - q % 2) + HALF * chunk
        src = feat.at[t // YB, :, pl.ds(pl.multiple_of(start_lane(q) + off, 128), HALF)]
        dst = arr.at[me, :, pl.ds(pl.multiple_of(off, 128), HALF)]
        return pltpu.make_async_remote_copy(
            src_ref=src, dst_ref=dst, send_sem=s_a.at[chunk, t], recv_sem=r_a.at[chunk, me],
            device_id=dev, device_id_type=MESH,
        )

    my_off = 128 * (1 - odd)
    own_in = pltpu.make_async_copy(
        feat.at[x, :, pl.ds(pl.multiple_of(start_lane(y) + my_off, 128), 2 * HALF)],
        arr.at[me, :, pl.ds(pl.multiple_of(my_off, 128), 2 * HALF)],
        l_a.at[0],
    )
    own_in.start()
    for chunk in range(2):

        def start_in(i, _):
            in_copy(i, chunk).start()
            return 0

        lax.fori_loop(1, 16, start_in, 0)

    for c in loads[1:]:
        c.wait()
    build_toeplitz(w2, wt2)

    def tap(i, _):
        rw[pl.ds(pl.multiple_of(128 * i, 128), CH), pl.ds(0, CH)] = wr[i]
        return 0

    lax.fori_loop(0, 9, tap, 0)
    for i in range(5):
        vec[i : i + 1, 0:CH] = vin[i]
    gain1, bias1, gain2, bias2, bias_r = [vec[i : i + 1] for i in range(5)]
    bias1w = jnp.concatenate([bias1, bias1], axis=1)
    gain2w = jnp.concatenate([gain2, gain2], axis=1)
    bias2w = jnp.concatenate([bias2, bias2], axis=1)

    own_in.wait()

    def wait_in(chunk):
        def step(i, _):
            t, dev = plane(i)
            dst = arr.at[t, :, pl.ds(pl.multiple_of(my_off + HALF * chunk, 128), HALF)]
            pltpu.make_async_remote_copy(
                src_ref=feat.at[0, :, pl.ds(0, HALF)], dst_ref=dst,
                send_sem=s_a.at[chunk, t], recv_sem=r_a.at[chunk, t],
                device_id=dev, device_id_type=MESH,
            ).wait_recv()
            return 0

        lax.fori_loop(1, 16, step, 0)

    lane = lax.broadcasted_iota(jnp.int32, (8, LANES), 1)
    sub8 = lax.broadcasted_iota(jnp.int32, (8, LANES), 0)
    frame128 = lax.broadcasted_iota(jnp.int32, (128, LANES), 0) % 16
    ones1 = jnp.ones((256, 128), BF16)

    def act_group(q, g):
        lane0 = pl.multiple_of(g * 384, 128)
        cols = [[] for _ in range(4)]
        for xb in range(XB):
            v = [arr[XB * xb + q, :, pl.ds(lane0 + 128 * m, 128)].astype(F32) for m in range(3)]
            cols[0].append(jnp.where(lane < 96, v[0], 0.0))
            cols[1].append(
                jnp.where(lane < 32, pltpu.roll(v[0], 32, 1), jnp.where(lane < 96, pltpu.roll(v[1], 32, 1), 0.0))
            )
            cols[2].append(
                jnp.where(lane < 64, pltpu.roll(v[1], 64, 1), jnp.where(lane < 96, pltpu.roll(v[2], 64, 1), 0.0))
            )
            cols[3].append(jnp.where(lane < 96, pltpu.roll(v[2], 96, 1), 0.0))
        tiles = []
        for c in cols:
            turned = [pltpu.roll(u, 4, 0) for u in c]
            tiles += [jnp.where(sub8 < 4, c[0], turned[1]), jnp.where(sub8 < 4, c[2], turned[3])]
            tiles += [jnp.where(sub8 < 4, turned[0], c[1]), jnp.where(sub8 < 4, turned[2], c[3])]
        return jnp.concatenate(tiles, axis=0)

    def act_store(flat, total, q, g):
        w0 = 4 * g
        row = 2 * q
        xs[pl.ds(w0, 4), pl.ds(row, 2)] = flat.astype(BF16).reshape(4, 2, 16, LANES)
        act = scaled_act(flat, total, gain1)
        for t in range(3):
            moved = act if t == 2 else shifted(act, 2 - t, frame128)
            a[t, pl.ds(w0, 4), pl.ds(row + 1, 2)] = moved.astype(BF16).reshape(4, 2, 16, LANES)

    def act_step(i, qs):
        flats = [act_group(q, i) for q in qs]
        hi, lo = split_square(jnp.concatenate(flats, axis=0))
        total = jnp.dot(jnp.concatenate([hi, lo], axis=1), ones1, preferred_element_type=F32)
        for m, q in enumerate(qs):
            act_store(flats[m], total[128 * m : 128 * m + 128], q, i)
        return 0

    def z_copy(src, dst, k, row):
        return pltpu.make_async_remote_copy(
            src_ref=src, dst_ref=dst, send_sem=s_z.at[k], recv_sem=r_z.at[k],
            device_id=(x, row, core), device_id_type=MESH,
        )

    inside = (z > 0, z < ZB - 1)

    def fill_halo(halo, dst, first, count, unit):
        frame = lax.broadcasted_iota(jnp.int32, (16 * unit, LANES), 0) % 16

        def step(i, _):
            c = first + unit * i
            for side in range(2):
                v = halo[side, pl.ds(c, unit)].astype(F32).reshape(16 * unit, LANES)
                v = jnp.where(inside[side], v, 0.0)
                for t in range(3):
                    moved = v if t == 2 else shifted(v, 2 - t, frame)
                    dst[t, pl.ds(c, unit), 9 * side] = moved.astype(BF16).reshape(unit, 16, LANES)
            return 0

        lax.fori_loop(0, count // unit, step, 0)

    base = 2 * (1 - odd)
    col0 = OWN * y

    def conv1(p0, pairs, rows):
        acc = jnp.dot(
            conv_lhs(a, base + 2 * p0, pairs, rows), wt1[...].reshape(4608, 256), preferred_element_type=F32
        )
        v = acc + bias1w
        hi, lo = split_square(v)
        total = jnp.dot(hi, ones2[...], preferred_element_type=F32) + jnp.dot(
            lo, ones2[...], preferred_element_type=F32
        )
        act = scaled_act(v, total, gain2w)
        height = sum(count for _, count in rows)
        m = 16 * height
        frame = lax.broadcasted_iota(jnp.int32, (m, LANES), 0) % 16
        for p in range(pairs):
            for n in range(2):
                bcol = 2 * (p0 + p) + n
                image = col0 - 1 + bcol
                u = act[m * p : m * p + m, 128 * n : 128 * n + 128]
                u = jnp.where(jnp.logical_and(image >= 0, image < 104), u, 0.0)
                for t in range(3):
                    moved = (u if t == 2 else shifted(u, 2 - t, frame)).astype(BF16)
                    at = 0
                    for first, count in rows:
                        b[t, bcol, first + 1 : first + 1 + count] = moved[16 * at : 16 * (at + count)].reshape(
                            count, 16, LANES
                        )
                        at += count

    def conv2(p0, pairs, rows):
        acc = jnp.dot(
            conv_lhs(b, 2 * p0, pairs, rows), wt2[...].reshape(4608, 256), preferred_element_type=F32
        )
        v = acc + bias2w
        height = sum(count for _, count in rows)
        m = 16 * height
        for p in range(pairs):
            for n in range(2):
                c = 2 * (p0 + p) + n
                u = v[m * p : m * p + m, 128 * n : 128 * n + 128]
                at = 0
                for first, count in rows:
                    part = u[16 * at : 16 * (at + count)]
                    part = part + xs[base + 2 + c, first : first + count].reshape(16 * count, LANES).astype(F32)
                    part = jnp.where(col0 + c < 104, part, 0.0)
                    ob[c, first : first + count] = part.astype(BF16).reshape(count, 16, LANES)
                    at += count

    CUT = (0, 16, 36)
    sends_a = []
    for chunk in range(2):
        wait_in(chunk)
        lo_w, hi_w = CUT[chunk], CUT[chunk + 1]
        lax.fori_loop(lo_w // 4, hi_w // 4, lambda i, _: act_step(i, (0, 3)), 0)
        part = pl.ds(lo_w, hi_w - lo_w)
        sends_a += [
            z_copy(a.at[2, part, 1], ha.at[1, part], 2 * chunk, up),
            z_copy(a.at[2, part, 8], ha.at[0, part], 2 * chunk + 1, down),
        ]
        sends_a[-2].start()
        sends_a[-1].start()
        lax.fori_loop(lo_w // 4, hi_w // 4, lambda i, _: act_step(i, (1, 2)), 0)

        def inner1(i, _):
            conv1(3 * i, 3, INNER)
            return 0

        lax.fori_loop(2 * chunk, 2 + 3 * chunk, inner1, 0)
    for c in sends_a:
        c.wait()
    fill_halo(ha, a, 0, WIN, 4)

    def edge1(i, _):
        conv1(5 * i, 5, EDGES)
        return 0

    lax.fori_loop(0, 3, edge1, 0)
    sends_b = [z_copy(b.at[2, :, 1], hb.at[1], 4, up), z_copy(b.at[2, :, 8], hb.at[0], 5, down)]
    for c in sends_b:
        c.start()

    def inner2(i, _):
        conv2(7 * i, 7, INNER)
        return 0

    lax.fori_loop(0, 2, inner2, 0)
    for c in sends_b:
        c.wait()
    fill_halo(hb, b, 0, BC, 5)
    conv2(0, PAIRS2, ((0, 1),))
    send_o = z_copy(ob.at[:, 0], ho, 6, up)
    send_o.start()
    conv2(0, PAIRS2, ((7, 1),))

    def reduce_rows(rows):
        pieces = []
        for j2 in range(3):
            for k in range(3):
                tiles = []
                for j in range(14):
                    c = min(2 * j + k, OC - 1)
                    tiles += [ob[c, 2 * i + j2] for i in rows]
                pieces.append(jnp.concatenate(tiles, axis=0))
        acc = jnp.dot(jnp.concatenate(pieces, axis=1), rw[...], preferred_element_type=F32) + bias_r
        m = 16 * len(rows)
        for n, i in enumerate(rows):
            for jj in range(7):
                for h in range(2):
                    at = 2 * jj * m + 16 * n + 8 * h
                    e, o = acc[at : at + 8], acc[at + m : at + m + 8]
                    sb[2 * h, i, jj] = jnp.where(sub8 < 4, e, pltpu.roll(o, 4, 0)).astype(BF16)
                    sb[2 * h + 1, i, jj] = jnp.where(sub8 < 4, pltpu.roll(e, 4, 0), o).astype(BF16)

    slot = XB * core + x

    def out_copy(i, k):
        xb = (x + k // 2) % XB
        c = (core + k) % 2
        return pltpu.make_async_remote_copy(
            src_ref=sb.at[xb, i], dst_ref=gb.at[slot, y], send_sem=s_g.at[i, k], recv_sem=r_g.at[slot, y],
            device_id=(xb, z * YB + i, c), device_id_type=MESH,
        )

    def start_out(i):
        def step(k, _):
            here = jnp.logical_and(k == 0, y == i)

            @pl.when(jnp.logical_not(here))
            def _():
                out_copy(i, k).start()

            return 0

        lax.fori_loop(0, 8, step, 0)

    reduce_rows((0, 1, 2))
    for i in range(3):
        start_out(i)
    send_o.wait()

    def fill_last(i, _):
        v = ho[pl.ds(7 * i, 7)].astype(F32)
        ob[pl.ds(7 * i, 7), 8] = jnp.where(z < ZB - 1, v, 0.0).astype(BF16)
        return 0

    lax.fori_loop(0, 4, fill_last, 0)
    reduce_rows((3,))
    start_out(3)
    own_out = pltpu.make_async_copy(sb.at[x, y], gb.at[slot, y], l_a.at[1])
    own_out.start()
    own_out.wait()

    def wait_out(k, _):
        s, q = k // YB, k % YB

        @pl.when(jnp.logical_not(jnp.logical_and(s == slot, q == y)))
        def _():
            pltpu.make_async_remote_copy(
                src_ref=sb.at[0, 0], dst_ref=gb.at[s, q], send_sem=s_g.at[0, 0], recv_sem=r_g.at[s, q],
                device_id=(x, zy, 1 - core), device_id_type=MESH,
            ).wait_recv()

        return 0

    lax.fori_loop(0, 32, wait_out, 0)

    def select(s, _):
        src = jnp.int32(0)
        length = jnp.int32(0)
        for c in range(8):
            hit = owner[c] == XB * core + s
            src = jnp.where(hit, stored[c], src)
            length = jnp.where(hit, lengths[c], length)
        alive = (XB * x + sub8 % 4) < length
        columns = []
        for q in range(YB):
            tiles = gb[src, q]
            for j in range(JC):
                tile = tiles[j // 2].astype(F32)
                columns.append(tile if j % 2 == 0 else pltpu.roll(tile, 4, 0))
        for g in range(13):
            c0, c1, c2, c3 = columns[4 * g : 4 * g + 4]
            t1, t2, t3 = pltpu.roll(c1, 96, 1), pltpu.roll(c2, 64, 1), pltpu.roll(c3, 32, 1)
            dense = [jnp.where(lane < 96, c0, t1), jnp.where(lane < 64, t1, t2), jnp.where(lane < 32, t2, t3)]
            for m in range(3):
                out[s, :, pl.ds(384 * g + 128 * m, 128)] = jnp.where(alive, dense[m], 0.0)[0:4].astype(BF16)
        return 0

    lax.fori_loop(0, XB, select, 0)

    def end_in(i, _):
        in_copy(i, 0).wait_send()
        in_copy(i, 1).wait_send()
        return 0

    lax.fori_loop(1, 16, end_in, 0)

    def end_out(k, _):
        for i in range(4):

            @pl.when(jnp.logical_not(jnp.logical_and(k == 0, y == i)))
            def _():
                out_copy(i, k).wait_send()

        return 0

    lax.fori_loop(0, 8, end_out, 0)


def local(
    features, lengths, stored_slot, owner_slot, gain_first, conv_first, bias_first,
    gain_second, conv_second, bias_second, reduce_conv_weight, reduce_conv_bias,
):
    slots, frames, rows, lanes = features.shape
    feat = jnp.transpose(features, (0, 2, 1, 3)).reshape(slots, rows * frames, lanes)
    feat = jnp.pad(feat, ((0, 0), (0, 0), (PADL, PADR)))
    hbm = pl.BlockSpec(memory_space=pltpu.HBM)
    dma = pltpu.SemaphoreType.DMA
    result = pl.pallas_call(
        kernel,
        out_shape=jax.ShapeDtypeStruct((slots, frames, 4992), BF16),
        in_specs=[pl.BlockSpec(memory_space=pl.ANY)] + [hbm] * 11,
        out_specs=pl.BlockSpec(memory_space=pltpu.VMEM),
        scratch_shapes=[
            pltpu.VMEM((16, 8, WIN * CH), BF16),
            pltpu.VMEM((WIN, 8, 16, LANES), BF16),
            pltpu.VMEM((3, WIN, 10, 16, LANES), BF16),
            pltpu.VMEM((3, BC, 10, 16, LANES), BF16),
            pltpu.VMEM((9, 512, 256), BF16),
            pltpu.VMEM((9, 512, 256), BF16),
            pltpu.VMEM((1152, 128), BF16),
            pltpu.VMEM((OC, 9, 16, LANES), BF16),
            pltpu.VMEM((XB, 4, 7, 8, LANES), BF16),
            pltpu.VMEM((2 * XB, YB, 7, 8, LANES), BF16),
            pltpu.VMEM((2, WIN, 16, LANES), BF16),
            pltpu.VMEM((2, BC, 16, LANES), BF16),
            pltpu.VMEM((OC, 16, LANES), BF16),
            pltpu.VMEM((27, CH, CH), BF16),
            pltpu.VMEM((27, CH, CH), BF16),
            pltpu.VMEM((9, CH, CH), BF16),
            pltpu.VMEM((5, 1, CH), F32),
            pltpu.VMEM((8, LANES), F32),
            pltpu.VMEM((256, 256), BF16),
            pltpu.SMEM((8,), jnp.int32),
            pltpu.SMEM((8,), jnp.int32),
            pltpu.SMEM((8,), jnp.int32),
            dma((2, 16)),
            dma((2, 16)),
            dma((7,)),
            dma((7,)),
            dma((4, 8)),
            dma((8, 4)),
            dma((2,)),
            dma((11,)),
        ],
        compiler_params=pltpu.CompilerParams(
            collective_id=0, has_side_effects=True, vmem_limit_bytes=50 << 20
        ),
        name="encode",
    )(
        feat,
        conv_first.reshape(27, CH, CH),
        conv_second.reshape(27, CH, CH),
        reduce_conv_weight.reshape(9, CH, CH),
        *[v.reshape(1, CH) for v in (gain_first, bias_first, gain_second, bias_second, reduce_conv_bias)],
        lengths, stored_slot, owner_slot,
    )
    return result.reshape(slots, frames, 1, 4992)


def solution(mesh):
    spec = P("clip", "tm", "rows", None)
    return jax.shard_map(
        local, mesh=mesh, in_specs=(spec,) + (P(),) * 11, out_specs=spec, check_vma=False
    )
```

time: 72.9 us -> 55.2 us (0.76)
  Pallas kernels: 67.7 us -> 51 us
  local copies, waits for them, and re-layouts: 4.94 us -> 3.39 us
    pallas_call x1, Pallas kernels: 67.7 us -> 51 us  [local(): pl.pallas_call(kernel, out_shape=jax.ShapeDtypeStruct((slots, frames, 499...]
    unnamed x23, local copies, waits for them, and re-layouts: 3.41 us -> 1.87 us
where the time goes in v1:
time: 55.2 us; the launch traced here: 54.5 us
  Pallas kernels  51 us (92%)
  local copies, waits for them, and re-layouts  3.39 us (6%)
    pallas_call x1, Pallas kernels, local(): pl.pallas_call(kernel, out_shape=jax.ShapeDtypeStruct((slots, frames, 499...  51 us
    unnamed x23, local copies, waits for them, and re-layouts  1.87 us
    transpose x1, local copies, waits for them, and re-layouts, local(): jnp.transpose(features, (0, 2, 1, 3)).reshape(slots, rows * frames, lanes)  1.33 us

profile of v1, /device:TPU:1, one launch (start us, length us, event | category | flops | bytes accessed | tf_op | source)
XLA Modules:
  0.0 54.5 jit_solution(17020523071600454028)
XLA Ops:
  0.0 1.3 %copy.13 = bf16[4,2,4,9984]{3,2,1,0:T(4,128)(2,1)S(1)} copy(bf16[4,2,4,9984]{3,1,2,0:T(2,128)(2,1)} %bitcast.21) | data formatting | bytes 1277952 | tf_op jit(solution)/shard_map/transpose | solution.py:480
  1.3 0.0 copy-start.2
  1.3 0.1 reshape.30
  1.5 0.0 copy-start
  1.5 0.0 copy-start.1
  1.5 0.0 copy-start.3
  1.5 0.0 copy-start.4
  1.5 0.0 copy-start.5
  1.6 0.0 copy-start.6
  1.6 0.0 copy-start.7
  1.6 0.0 copy-start.8
  1.6 0.0 copy-start.9
  1.6 0.0 copy-start.10
  1.6 0.1 pad.4.feat
  1.7 0.6 %copy-done.2 = bf16[3,3,96,96]{3,2,1,0:T(8,128)(2,1)S(1)} copy-done((bf16[3,3,96,96]{3,2,1,0:T(8,128)(2,1)S(1)}, bf16[3,3,96,96]{3,2,1,0:T(8,128)(2,1)}, u32[]{:S(2)}) %copy-start.2) | copy-done | bytes 165912
  2.3 0.3 copy-done
  2.6 0.2 copy-done.1
  2.8 0.0 copy-done.3
  2.8 0.0 copy-done.4
  2.8 0.0 copy-done.5
  2.8 0.0 copy-done.6
  2.8 0.0 copy-done.7
  2.8 0.0 copy-done.8
  2.8 0.0 copy-done.9
  2.9 0.0 copy-done.10
  2.9 51.0 %encode.1 = bf16[4,4,4992]{2,1,0:T(4,128)(2,1)S(1)} custom-call(bf16[4,8,11136]{2,1,0:T(8,128)(2,1)S(1)} %pad.4.feat, bf16[27,96,96]{2,1,0:T(8,128)(2,1)S(1)} %bitcast.12, bf16[27,96,96]{2,1,0:T(8,128)(2,1)S(1)} %bitcast.13, bf16[9,96,96]{2,1,0:T(8,128)(2,1)S(1)} %bitcast.15, f32[1,96]{1,0:T(1,128)S(1)} %bitcast.16, f32[1,96]{1,0:T(1,128)S(1)} %bitcast.17, ...), custom_call_target="tpu_custom_call" | custom-call | tf_op jit(solution)/shard_map/encode/pallas_call | solution.py:484
  53.8 0.7 %copy.16 = bf16[4,4,1,4992]{3,1,2,0:T(4,128)(2,1)} copy(bf16[4,4,1,4992]{3,1,2,0:T(4,128)(2,1)S(1)} %bitcast.14) | data formatting | bytes 319488
Async XLA Ops:
  1.3 0.9 %copy-start.2 = (bf16[3,3,96,96]{3,2,1,0:T(8,128)(2,1)S(1)}, bf16[3,3,96,96]{3,2,1,0:T(8,128)(2,1)}, u32[]{:S(2)}) copy-start(bf16[3,3,96,96]{3,2,1,0:T(8,128)(2,1)} %param.22) | copy-start | bytes 497668
  1.5 1.1 %copy-start = (bf16[3,3,3,96,96]{4,3,2,1,0:T(8,128)(2,1)S(1)}, bf16[3,3,3,96,96]{4,3,2,1,0:T(8,128)(2,1)}, u32[]{:S(2)}) copy-start(bf16[3,3,3,96,96]{4,3,2,1,0:T(8,128)(2,1)} %param.17) | copy-start | bytes 1492996
  1.5 1.3 %copy-start.1 = (bf16[3,3,3,96,96]{4,3,2,1,0:T(8,128)(2,1)S(1)}, bf16[3,3,3,96,96]{4,3,2,1,0:T(8,128)(2,1)}, u32[]{:S(2)}) copy-start(bf16[3,3,3,96,96]{4,3,2,1,0:T(8,128)(2,1)} %param.20) | copy-start | bytes 1492996
  1.5 1.3 %copy-start.3 = (f32[96]{0:T(128)S(1)}, f32[96]{0:T(128)}, u32[]{:S(2)}) copy-start(f32[96]{0:T(128)} %param.16) | copy-start | bytes 1156
  1.5 1.3 %copy-start.4 = (f32[96]{0:T(128)S(1)}, f32[96]{0:T(128)}, u32[]{:S(2)}) copy-start(f32[96]{0:T(128)} %param.18) | copy-start | bytes 1156
  1.5 1.3 %copy-start.5 = (f32[96]{0:T(128)S(1)}, f32[96]{0:T(128)}, u32[]{:S(2)}) copy-start(f32[96]{0:T(128)} %param.19) | copy-start | bytes 1156
  1.6 1.3 %copy-start.6 = (f32[96]{0:T(128)S(1)}, f32[96]{0:T(128)}, u32[]{:S(2)}) copy-start(f32[96]{0:T(128)} %param.21) | copy-start | bytes 1156
  1.6 1.3 %copy-start.7 = (f32[96]{0:T(128)S(1)}, f32[96]{0:T(128)}, u32[]{:S(2)}) copy-start(f32[96]{0:T(128)} %param.23) | copy-start | bytes 1156
  1.6 1.3 %copy-start.8 = (s32[8]{0:T(128)S(1)}, s32[8]{0:T(128)}, u32[]{:S(2)}) copy-start(s32[8]{0:T(128)} %lenh.1) | copy-start | bytes 100
  1.6 1.3 %copy-start.9 = (s32[8]{0:T(128)S(1)}, s32[8]{0:T(128)}, u32[]{:S(2)}) copy-start(s32[8]{0:T(128)} %stoh.1) | copy-start | bytes 100
  1.6 1.3 %copy-start.10 = (s32[8]{0:T(128)S(1)}, s32[8]{0:T(128)}, u32[]{:S(2)}) copy-start(s32[8]{0:T(128)} %ownh.1) | copy-start | bytes 100

commit v2 on v1

--- a/solution.py
+++ b/solution.py
@@ -31,18 +31,13 @@
     return jnp.where(frame < step, 0.0, pltpu.roll(flat, step, 0))
 
 
-def silu(u):
-    return 0.5 * u * (1.0 + jnp.tanh(0.5 * u))
-
-
-def split_square(v):
-    sq = v * v
-    hi = sq.astype(BF16)
-    return hi, (sq - hi.astype(F32)).astype(BF16)
-
-
-def scaled_act(v, total, gain):
-    return silu(v * lax.rsqrt(total * (1.0 / CH) + NORM_EPS) * gain)
+def square(v):
+    return (v * v).astype(BF16)
+
+
+def scaled_act(v, total, half_gain):
+    half = v * lax.rsqrt(total * (1.0 / CH) + NORM_EPS) * half_gain
+    return half + half * jnp.tanh(half)
 
 
 def build_toeplitz(w_ref, wt):
@@ -98,17 +93,15 @@
     arr[:, :, 3072:3456] = jnp.zeros((16, 8, 384), BF16)
     barrier = pltpu.get_barrier_semaphore()
 
-    def greet(i, _):
-        t = (me + i) % 16
-        c = (core + i // 16) % 2
-        pl.semaphore_signal(
-            barrier, inc=1, device_id=(t // YB, z * YB + t % YB, c), device_id_type=MESH
-        )
-        return 0
-
-    lax.fori_loop(1, 32, greet, 0)
-    for row in (up, down):
-        pl.semaphore_signal(barrier, inc=1, device_id=(x, row, core), device_id_type=MESH)
+    xs_of = [(x + d) % XB for d in range(XB)]
+    ys_of = [(y + d) % YB for d in range(YB)]
+    for dx in range(XB):
+        for dy in range(YB):
+            if dx or dy:
+                dev = (xs_of[dx], z * YB + ys_of[dy], core)
+                pl.semaphore_signal(barrier, inc=1, device_id=dev, device_id_type=MESH)
+    for dev in ((x, up, core), (x, down, core), (x, zy, 1 - core)):
+        pl.semaphore_signal(barrier, inc=1, device_id=dev, device_id_type=MESH)
 
     loads = [
         pltpu.make_async_copy(src, dst, l_w.at[i])
@@ -134,9 +127,9 @@
     ones2[...] = jnp.where(r_i == c_i, 1.0, 0.0).astype(BF16)
     loads[0].wait()
     build_toeplitz(w1, wt1)
-    pl.semaphore_wait(barrier, 33)
-
-    HALF = 1536
+    pl.semaphore_wait(barrier, 18)
+
+    HALF = 1024
     odd = y % 2
 
     def in_copy(i, chunk):
@@ -152,12 +145,12 @@
 
     my_off = 128 * (1 - odd)
     own_in = pltpu.make_async_copy(
-        feat.at[x, :, pl.ds(pl.multiple_of(start_lane(y) + my_off, 128), 2 * HALF)],
-        arr.at[me, :, pl.ds(pl.multiple_of(my_off, 128), 2 * HALF)],
+        feat.at[x, :, pl.ds(pl.multiple_of(start_lane(y) + my_off, 128), 3 * HALF)],
+        arr.at[me, :, pl.ds(pl.multiple_of(my_off, 128), 3 * HALF)],
         l_a.at[0],
     )
     own_in.start()
-    for chunk in range(2):
+    for chunk in range(3):
 
         def start_in(i, _):
             in_copy(i, chunk).start()
@@ -177,6 +170,7 @@
     for i in range(5):
         vec[i : i + 1, 0:CH] = vin[i]
     gain1, bias1, gain2, bias2, bias_r = [vec[i : i + 1] for i in range(5)]
+    gain1, gain2 = 0.5 * gain1, 0.5 * gain2
     bias1w = jnp.concatenate([bias1, bias1], axis=1)
     gain2w = jnp.concatenate([gain2, gain2], axis=1)
     bias2w = jnp.concatenate([bias2, bias2], axis=1)
@@ -199,7 +193,6 @@
     lane = lax.broadcasted_iota(jnp.int32, (8, LANES), 1)
     sub8 = lax.broadcasted_iota(jnp.int32, (8, LANES), 0)
     frame128 = lax.broadcasted_iota(jnp.int32, (128, LANES), 0) % 16
-    ones1 = jnp.ones((256, 128), BF16)
 
     def act_group(q, g):
         lane0 = pl.multiple_of(g * 384, 128)
@@ -232,10 +225,10 @@
 
     def act_step(i, qs):
         flats = [act_group(q, i) for q in qs]
-        hi, lo = split_square(jnp.concatenate(flats, axis=0))
-        total = jnp.dot(jnp.concatenate([hi, lo], axis=1), ones1, preferred_element_type=F32)
+        both = jnp.concatenate([square(u) for u in flats], axis=1)
+        total = jnp.dot(both, ones2[...], preferred_element_type=F32)
         for m, q in enumerate(qs):
-            act_store(flats[m], total[128 * m : 128 * m + 128], q, i)
+            act_store(flats[m], total[:, 128 * m : 128 * m + 128], q, i)
         return 0
 
     def z_copy(src, dst, k, row):
@@ -269,10 +262,7 @@
             conv_lhs(a, base + 2 * p0, pairs, rows), wt1[...].reshape(4608, 256), preferred_element_type=F32
         )
         v = acc + bias1w
-        hi, lo = split_square(v)
-        total = jnp.dot(hi, ones2[...], preferred_element_type=F32) + jnp.dot(
-            lo, ones2[...], preferred_element_type=F32
-        )
+        total = jnp.dot(square(v), ones2[...], preferred_element_type=F32)
         act = scaled_act(v, total, gain2w)
         height = sum(count for _, count in rows)
         m = 16 * height
@@ -311,9 +301,15 @@
                     ob[c, first : first + count] = part.astype(BF16).reshape(count, 16, LANES)
                     at += count
 
-    CUT = (0, 16, 36)
+    CUT = (0, 8, 20, 36)
+    INNER_CUT = (0, 0, 2, 5)
+
+    def inner1(i, _):
+        conv1(3 * i, 3, INNER)
+        return 0
+
     sends_a = []
-    for chunk in range(2):
+    for chunk in range(3):
         wait_in(chunk)
         lo_w, hi_w = CUT[chunk], CUT[chunk + 1]
         lax.fori_loop(lo_w // 4, hi_w // 4, lambda i, _: act_step(i, (0, 3)), 0)
@@ -325,37 +321,31 @@
         sends_a[-2].start()
         sends_a[-1].start()
         lax.fori_loop(lo_w // 4, hi_w // 4, lambda i, _: act_step(i, (1, 2)), 0)
-
-        def inner1(i, _):
-            conv1(3 * i, 3, INNER)
-            return 0
-
-        lax.fori_loop(2 * chunk, 2 + 3 * chunk, inner1, 0)
+        if INNER_CUT[chunk] < INNER_CUT[chunk + 1]:
+            lax.fori_loop(INNER_CUT[chunk], INNER_CUT[chunk + 1], inner1, 0)
     for c in sends_a:
         c.wait()
     fill_halo(ha, a, 0, WIN, 4)
 
-    def edge1(i, _):
-        conv1(5 * i, 5, EDGES)
-        return 0
-
-    lax.fori_loop(0, 3, edge1, 0)
-    sends_b = [z_copy(b.at[2, :, 1], hb.at[1], 4, up), z_copy(b.at[2, :, 8], hb.at[0], 5, down)]
-    for c in sends_b:
-        c.start()
-
-    def inner2(i, _):
-        conv2(7 * i, 7, INNER)
-        return 0
-
-    lax.fori_loop(0, 2, inner2, 0)
+    sends_b = []
+    for e in range(3):
+        conv1(5 * e, 5, EDGES)
+        part = pl.ds(10 * e, 10)
+        sends_b += [
+            z_copy(b.at[2, part, 1], hb.at[1, part], 6 + 2 * e, up),
+            z_copy(b.at[2, part, 8], hb.at[0, part], 7 + 2 * e, down),
+        ]
+        sends_b[-2].start()
+        sends_b[-1].start()
+
+    conv2(0, 7, INNER)
     for c in sends_b:
         c.wait()
     fill_halo(hb, b, 0, BC, 5)
     conv2(0, PAIRS2, ((0, 1),))
-    send_o = z_copy(ob.at[:, 0], ho, 6, up)
+    send_o = z_copy(ob.at[:, 0], ho, 12, up)
     send_o.start()
-    conv2(0, PAIRS2, ((7, 1),))
+    conv2(7, 7, INNER)
 
     def reduce_rows(rows):
         pieces = []
@@ -386,6 +376,15 @@
             device_id=(xb, z * YB + i, c), device_id_type=MESH,
         )
 
+    def end_out(k, _):
+        for i in range(4):
+
+            @pl.when(jnp.logical_not(jnp.logical_and(k == 0, y == i)))
+            def _():
+                out_copy(i, k).wait_send()
+
+        return 0
+
     def start_out(i):
         def step(k, _):
             here = jnp.logical_and(k == 0, y == i)
@@ -398,9 +397,12 @@
 
         lax.fori_loop(0, 8, step, 0)
 
-    reduce_rows((0, 1, 2))
-    for i in range(3):
-        start_out(i)
+    reduce_rows((1, 2))
+    start_out(1)
+    start_out(2)
+    conv2(0, PAIRS2, ((7, 1),))
+    reduce_rows((0,))
+    start_out(0)
     send_o.wait()
 
     def fill_last(i, _):
@@ -454,20 +456,11 @@
     lax.fori_loop(0, XB, select, 0)
 
     def end_in(i, _):
-        in_copy(i, 0).wait_send()
-        in_copy(i, 1).wait_send()
+        for chunk in range(3):
+            in_copy(i, chunk).wait_send()
         return 0
 
     lax.fori_loop(1, 16, end_in, 0)
-
-    def end_out(k, _):
-        for i in range(4):
-
-            @pl.when(jnp.logical_not(jnp.logical_and(k == 0, y == i)))
-            def _():
-                out_copy(i, k).wait_send()
-
-        return 0
 
     lax.fori_loop(0, 8, end_out, 0)
 
@@ -509,17 +502,17 @@
             pltpu.SMEM((8,), jnp.int32),
             pltpu.SMEM((8,), jnp.int32),
             pltpu.SMEM((8,), jnp.int32),
-            dma((2, 16)),
-            dma((2, 16)),
-            dma((7,)),
-            dma((7,)),
+            dma((3, 16)),
+            dma((3, 16)),
+            dma((13,)),
+            dma((13,)),
             dma((4, 8)),
             dma((8, 4)),
             dma((2,)),
             dma((11,)),
         ],
         compiler_params=pltpu.CompilerParams(
-            collective_id=0, has_side_effects=True, vmem_limit_bytes=50 << 20
+            collective_id=0, has_side_effects=True, vmem_limit_bytes=60 << 20
         ),
         name="encode",
     )(

time: 55.2 us -> 57.6 us (1.043); the launches traced: 54.5 us -> 57.5 us
  Pallas kernels: 51 us -> 53.5 us
  local copies, waits for them, and re-layouts: 3.39 us -> 4.01 us
    pallas_call x1, Pallas kernels: 51 us -> 53.5 us  [local(): pl.pallas_call(kernel, out_shape=jax.ShapeDtypeStruct((slots, frames, 499...]
    pad x1, local copies, waits for them, and re-layouts: 0.05 us -> 0.9 us  [local(): feat = jnp.pad(feat, ((0, 0), (0, 0), (PADL, PADR)))]
    unnamed x23 -> x1, local copies, waits for them, and re-layouts: 1.87 us -> 1.64 us
where the time goes in v2:
time: 57.6 us; the launch traced here: 57.5 us
  Pallas kernels  53.5 us (93%)
  local copies, waits for them, and re-layouts  4.01 us (7%)
    pallas_call x1, Pallas kernels, local(): pl.pallas_call(kernel, out_shape=jax.ShapeDtypeStruct((slots, frames, 499...  53.5 us
    unnamed x1, local copies, waits for them, and re-layouts  1.64 us
    transpose x1, local copies, waits for them, and re-layouts, local(): jnp.transpose(features, (0, 2, 1, 3)).reshape(slots, rows * frames, lanes)  1.33 us

profile of v2, /device:TPU:1, one launch (start us, length us, event | category | flops | bytes accessed | tf_op | source)
XLA Modules:
  0.0 57.5 jit_solution(747685195378576332)
XLA Ops:
  0.0 1.3 %copy.13 = bf16[4,2,4,9984]{3,2,1,0:T(4,128)(2,1)S(1)} copy(bf16[4,2,4,9984]{3,1,2,0:T(2,128)(2,1)} %bitcast.15) | data formatting | bytes 1277952 | tf_op jit(solution)/shard_map/transpose | solution.py:473
  1.3 0.1 reshape.30
  1.5 0.9 %pad.4.feat = bf16[4,8,11136]{2,1,0:T(8,128)(2,1)} pad(bf16[4,8,9984]{2,1,0:T(8,128)(2,1)S(1)} %reshape.30, bf16[]{:T(256)} %constant.2.clone.1), padding=0_0x0_0x384_768 | pad | bytes 1351682 | tf_op jit(solution)/shard_map/jit(_pad)/pad | solution.py:474
  2.4 53.5 %encode.1 = bf16[4,4,4992]{2,1,0:T(4,128)(2,1)} custom-call(bf16[4,8,11136]{2,1,0:T(8,128)(2,1)} %pad.4.feat, bf16[27,96,96]{2,1,0:T(8,128)(2,1)} %bitcast.12, bf16[27,96,96]{2,1,0:T(8,128)(2,1)} %bitcast.13, bf16[9,96,96]{2,1,0:T(8,128)(2,1)} %bitcast.16, f32[1,96]{1,0:T(1,128)} %bitcast.17, f32[1,96]{1,0:T(1,128)} %bitcast.18, f32[1,96]{1,0:T(1,128)} %bitcast.19, ...), custom_call_target="tpu_custom_call" | custom-call | tf_op jit(solution)/shard_map/encode/pallas_call | solution.py:477
  55.9 1.6 %copy.16 = bf16[4,4,1,4992]{3,1,2,0:T(4,128)(2,1)} copy(bf16[4,4,1,4992]{3,1,2,0:T(4,128)(2,1)} %bitcast.14) | data formatting | bytes 319488

commit v3 on v2

--- a/solution.py
+++ b/solution.py
@@ -31,8 +31,10 @@
     return jnp.where(frame < step, 0.0, pltpu.roll(flat, step, 0))
 
 
-def square(v):
-    return (v * v).astype(BF16)
+def split_square(v):
+    sq = v * v
+    hi = sq.astype(BF16)
+    return hi, (sq - hi.astype(F32)).astype(BF16)
 
 
 def scaled_act(v, total, half_gain):
@@ -66,11 +68,12 @@
 
 INNER = ((1, 6),)
 EDGES = ((0, 1), (7, 1))
+EDGES2 = ((0, 1), (7, 2))
 
 
 def kernel(
     feat, w1h, w2h, wrh, g1h, b1h, g2h, b2h, brh, lenh, stoh, ownh, out,
-    arr, xs, a, b, wt1, wt2, rw, ob, sb, gb, ha, hb, ho, w1, w2, wr, vin, vec, ones2,
+    arr, xs, a, b, wt1, wt2, rw, ob, sb, gb, ha, hb, w1, w2, wr, vin, vec, ones2,
     lengths, stored, owner,
     s_a, r_a, s_z, r_z, s_g, r_g, l_a, l_w,
 ):
@@ -150,13 +153,12 @@
         l_a.at[0],
     )
     own_in.start()
-    for chunk in range(3):
-
-        def start_in(i, _):
-            in_copy(i, chunk).start()
-            return 0
-
-        lax.fori_loop(1, 16, start_in, 0)
+
+    def start_in(i, _):
+        in_copy(i % 15 + 1, i // 15).start()
+        return 0
+
+    lax.fori_loop(0, 45, start_in, 0)
 
     for c in loads[1:]:
         c.wait()
@@ -192,6 +194,7 @@
 
     lane = lax.broadcasted_iota(jnp.int32, (8, LANES), 1)
     sub8 = lax.broadcasted_iota(jnp.int32, (8, LANES), 0)
+    ones1 = jnp.ones((256, LANES), BF16)
     frame128 = lax.broadcasted_iota(jnp.int32, (128, LANES), 0) % 16
 
     def act_group(q, g):
@@ -225,10 +228,10 @@
 
     def act_step(i, qs):
         flats = [act_group(q, i) for q in qs]
-        both = jnp.concatenate([square(u) for u in flats], axis=1)
-        total = jnp.dot(both, ones2[...], preferred_element_type=F32)
+        hi, lo = split_square(jnp.concatenate(flats, axis=0))
+        total = jnp.dot(jnp.concatenate([hi, lo], axis=1), ones1, preferred_element_type=F32)
         for m, q in enumerate(qs):
-            act_store(flats[m], total[:, 128 * m : 128 * m + 128], q, i)
+            act_store(flats[m], total[128 * m : 128 * m + 128], q, i)
         return 0
 
     def z_copy(src, dst, k, row):
@@ -239,17 +242,17 @@
 
     inside = (z > 0, z < ZB - 1)
 
-    def fill_halo(halo, dst, first, count, unit):
+    def fill_halo(halo, dst, count, unit, sides):
         frame = lax.broadcasted_iota(jnp.int32, (16 * unit, LANES), 0) % 16
 
         def step(i, _):
-            c = first + unit * i
-            for side in range(2):
+            c = unit * i
+            for side, row in enumerate(sides):
                 v = halo[side, pl.ds(c, unit)].astype(F32).reshape(16 * unit, LANES)
-                v = jnp.where(inside[side], v, 0.0)
+                v = jnp.where(inside[min(side, 1)], v, 0.0)
                 for t in range(3):
                     moved = v if t == 2 else shifted(v, 2 - t, frame)
-                    dst[t, pl.ds(c, unit), 9 * side] = moved.astype(BF16).reshape(unit, 16, LANES)
+                    dst[t, pl.ds(c, unit), row] = moved.astype(BF16).reshape(unit, 16, LANES)
             return 0
 
         lax.fori_loop(0, count // unit, step, 0)
@@ -262,7 +265,10 @@
             conv_lhs(a, base + 2 * p0, pairs, rows), wt1[...].reshape(4608, 256), preferred_element_type=F32
         )
         v = acc + bias1w
-        total = jnp.dot(square(v), ones2[...], preferred_element_type=F32)
+        hi, lo = split_square(v)
+        total = jnp.dot(hi, ones2[...], preferred_element_type=F32) + jnp.dot(
+            lo, ones2[...], preferred_element_type=F32
+        )
         act = scaled_act(v, total, gain2w)
         height = sum(count for _, count in rows)
         m = 16 * height
@@ -297,55 +303,76 @@
                 for first, count in rows:
                     part = u[16 * at : 16 * (at + count)]
                     part = part + xs[base + 2 + c, first : first + count].reshape(16 * count, LANES).astype(F32)
-                    part = jnp.where(col0 + c < 104, part, 0.0)
-                    ob[c, first : first + count] = part.astype(BF16).reshape(count, 16, LANES)
+                    part = jnp.where(col0 + c < 104, part, 0.0).astype(BF16).reshape(count, 16, LANES)
+                    if first + count == 9:
+                        ob[c, first : first + count - 1] = part[: count - 1]
+                        ob[c, 8:9] = jnp.where(z < ZB - 1, part[count - 1 :], 0.0).astype(BF16)
+                    else:
+                        ob[c, first : first + count] = part
                     at += count
-
-    CUT = (0, 8, 20, 36)
-    INNER_CUT = (0, 0, 2, 5)
 
     def inner1(i, _):
         conv1(3 * i, 3, INNER)
         return 0
 
-    sends_a = []
-    for chunk in range(3):
+    def a_copies(g):
+        part = pl.ds(4 * g, 4)
+        return (
+            z_copy(a.at[2, part, 1], ha.at[1, part], g, up),
+            z_copy(a.at[2, part, 8], ha.at[0, part], 9 + g, down),
+            z_copy(xs.at[part, 0], xs.at[part, 8], 18 + g, up),
+        )
+
+    def outer_rows(g, _):
+        act_step(g, (0, 3))
+        for c in a_copies(g):
+            c.start()
+        return 0
+
+    def inner_rows(g, _):
+        return act_step(g, (1, 2))
+
+    def chunk_step(chunk, _):
         wait_in(chunk)
-        lo_w, hi_w = CUT[chunk], CUT[chunk + 1]
-        lax.fori_loop(lo_w // 4, hi_w // 4, lambda i, _: act_step(i, (0, 3)), 0)
-        part = pl.ds(lo_w, hi_w - lo_w)
-        sends_a += [
-            z_copy(a.at[2, part, 1], ha.at[1, part], 2 * chunk, up),
-            z_copy(a.at[2, part, 8], ha.at[0, part], 2 * chunk + 1, down),
-        ]
-        sends_a[-2].start()
-        sends_a[-1].start()
-        lax.fori_loop(lo_w // 4, hi_w // 4, lambda i, _: act_step(i, (1, 2)), 0)
-        if INNER_CUT[chunk] < INNER_CUT[chunk + 1]:
-            lax.fori_loop(INNER_CUT[chunk], INNER_CUT[chunk + 1], inner1, 0)
-    for c in sends_a:
-        c.wait()
-    fill_halo(ha, a, 0, WIN, 4)
-
-    sends_b = []
-    for e in range(3):
+        g0, g1 = chunk * (chunk + 3) // 2, (chunk + 1) * (chunk + 4) // 2
+        lax.fori_loop(g0, g1, outer_rows, 0)
+        lax.fori_loop(g0, g1, inner_rows, 0)
+        p0 = jnp.maximum(chunk - 1, 0)
+        lax.fori_loop(p0 * (p0 + 3) // 2, chunk * (chunk + 3) // 2, inner1, 0)
+        return 0
+
+    lax.fori_loop(0, 3, chunk_step, 0)
+    early_b = z_copy(b.at[2, :, 2], hb.at[2], 33, up)
+    early_b.start()
+
+    def end_a(g, _):
+        for c in a_copies(g):
+            c.wait()
+        return 0
+
+    lax.fori_loop(0, GROUPS, end_a, 0)
+    fill_halo(ha, a, WIN, 4, (0, 9))
+
+    def b_copies(e):
+        part = pl.ds(10 * e, 10)
+        return (
+            z_copy(b.at[2, part, 1], hb.at[1, part], 27 + e, up),
+            z_copy(b.at[2, part, 8], hb.at[0, part], 30 + e, down),
+        )
+
+    def edge1(e, _):
         conv1(5 * e, 5, EDGES)
-        part = pl.ds(10 * e, 10)
-        sends_b += [
-            z_copy(b.at[2, part, 1], hb.at[1, part], 6 + 2 * e, up),
-            z_copy(b.at[2, part, 8], hb.at[0, part], 7 + 2 * e, down),
-        ]
-        sends_b[-2].start()
-        sends_b[-1].start()
-
-    conv2(0, 7, INNER)
-    for c in sends_b:
-        c.wait()
-    fill_halo(hb, b, 0, BC, 5)
-    conv2(0, PAIRS2, ((0, 1),))
-    send_o = z_copy(ob.at[:, 0], ho, 12, up)
-    send_o.start()
-    conv2(7, 7, INNER)
+        for c in b_copies(e):
+            c.start()
+        return 0
+
+    lax.fori_loop(0, 3, edge1, 0)
+
+    def inner2(i, _):
+        conv2(7 * i, 7, INNER)
+        return 0
+
+    lax.fori_loop(0, 2, inner2, 0)
 
     def reduce_rows(rows):
         pieces = []
@@ -400,18 +427,23 @@
     reduce_rows((1, 2))
     start_out(1)
     start_out(2)
-    conv2(0, PAIRS2, ((7, 1),))
-    reduce_rows((0,))
+    early_b.wait()
+
+    def end_b(e, _):
+        for c in b_copies(e):
+            c.wait()
+        return 0
+
+    lax.fori_loop(0, 3, end_b, 0)
+    fill_halo(hb, b, BC, 5, (0, 9, 10))
+
+    def edge2(i, _):
+        conv2(7 * i, 7, EDGES2)
+        return 0
+
+    lax.fori_loop(0, 2, edge2, 0)
+    reduce_rows((0, 3))
     start_out(0)
-    send_o.wait()
-
-    def fill_last(i, _):
-        v = ho[pl.ds(7 * i, 7)].astype(F32)
-        ob[pl.ds(7 * i, 7), 8] = jnp.where(z < ZB - 1, v, 0.0).astype(BF16)
-        return 0
-
-    lax.fori_loop(0, 4, fill_last, 0)
-    reduce_rows((3,))
     start_out(3)
     own_out = pltpu.make_async_copy(sb.at[x, y], gb.at[slot, y], l_a.at[1])
     own_out.start()
@@ -481,9 +513,9 @@
         out_specs=pl.BlockSpec(memory_space=pltpu.VMEM),
         scratch_shapes=[
             pltpu.VMEM((16, 8, WIN * CH), BF16),
-            pltpu.VMEM((WIN, 8, 16, LANES), BF16),
+            pltpu.VMEM((WIN, 9, 16, LANES), BF16),
             pltpu.VMEM((3, WIN, 10, 16, LANES), BF16),
-            pltpu.VMEM((3, BC, 10, 16, LANES), BF16),
+            pltpu.VMEM((3, BC, 11, 16, LANES), BF16),
             pltpu.VMEM((9, 512, 256), BF16),
             pltpu.VMEM((9, 512, 256), BF16),
             pltpu.VMEM((1152, 128), BF16),
@@ -491,8 +523,7 @@
             pltpu.VMEM((XB, 4, 7, 8, LANES), BF16),
             pltpu.VMEM((2 * XB, YB, 7, 8, LANES), BF16),
             pltpu.VMEM((2, WIN, 16, LANES), BF16),
-            pltpu.VMEM((2, BC, 16, LANES), BF16),
-            pltpu.VMEM((OC, 16, LANES), BF16),
+            pltpu.VMEM((3, BC, 16, LANES), BF16),
             pltpu.VMEM((27, CH, CH), BF16),
             pltpu.VMEM((27, CH, CH), BF16),
             pltpu.VMEM((9, CH, CH), BF16),
@@ -504,15 +535,15 @@
             pltpu.SMEM((8,), jnp.int32),
             dma((3, 16)),
             dma((3, 16)),
-            dma((13,)),
-            dma((13,)),
+            dma((34,)),
+            dma((34,)),
             dma((4, 8)),
             dma((8, 4)),
             dma((2,)),
             dma((11,)),
         ],
         compiler_params=pltpu.CompilerParams(
-            collective_id=0, has_side_effects=True, vmem_limit_bytes=60 << 20
+            collective_id=0, has_side_effects=True, vmem_limit_bytes=50 << 20
         ),
         name="encode",
     )(

time: 57.6 us -> 52.9 us (0.918)
  Pallas kernels: 53.5 us -> 49.2 us
  local copies, waits for them, and re-layouts: 4.01 us -> 3.39 us
    pallas_call x1, Pallas kernels: 53.5 us -> 49.2 us  [local(): pl.pallas_call(kernel, out_shape=jax.ShapeDtypeStruct((slots, frames, 499...]
    pad x1, local copies, waits for them, and re-layouts: 0.9 us -> 0.05 us  [local(): feat = jnp.pad(feat, ((0, 0), (0, 0), (PADL, PADR)))]
    unnamed x1 -> x23, local copies, waits for them, and re-layouts: 1.64 us -> 1.87 us
where the time goes in v3:
time: 52.9 us; the launch traced here: 52.8 us
  Pallas kernels  49.2 us (93%)
  local copies, waits for them, and re-layouts  3.39 us (6%)
    pallas_call x1, Pallas kernels, local(): pl.pallas_call(kernel, out_shape=jax.ShapeDtypeStruct((slots, frames, 499...  49.2 us
    unnamed x23, local copies, waits for them, and re-layouts  1.87 us
    transpose x1, local copies, waits for them, and re-layouts, local(): jnp.transpose(features, (0, 2, 1, 3)).reshape(slots, rows * frames, lanes)  1.33 us

profile of v3, /device:TPU:1, one launch (start us, length us, event | category | flops | bytes accessed | tf_op | source)
XLA Modules:
  0.0 52.8 jit_solution(18419953880232865198)
XLA Ops:
  0.0 1.3 %copy.13 = bf16[4,2,4,9984]{3,2,1,0:T(4,128)(2,1)S(1)} copy(bf16[4,2,4,9984]{3,1,2,0:T(2,128)(2,1)} %bitcast.21) | data formatting | bytes 1277952 | tf_op jit(solution)/shard_map/transpose | solution.py:505
  1.3 0.0 copy-start.2
  1.3 0.1 reshape.30
  1.5 0.0 copy-start
  1.5 0.0 copy-start.1
  1.5 0.0 copy-start.3
  1.5 0.0 copy-start.4
  1.5 0.0 copy-start.5
  1.6 0.0 copy-start.6
  1.6 0.0 copy-start.7
  1.6 0.0 copy-start.8
  1.6 0.0 copy-start.9
  1.6 0.0 copy-start.10
  1.6 0.1 pad.4.feat
  1.7 0.6 %copy-done.2 = bf16[3,3,96,96]{3,2,1,0:T(8,128)(2,1)S(1)} copy-done((bf16[3,3,96,96]{3,2,1,0:T(8,128)(2,1)S(1)}, bf16[3,3,96,96]{3,2,1,0:T(8,128)(2,1)}, u32[]{:S(2)}) %copy-start.2) | copy-done | bytes 165912
  2.3 0.3 copy-done
  2.6 0.2 copy-done.1
  2.8 0.0 copy-done.3
  2.8 0.0 copy-done.4
  2.8 0.0 copy-done.5
  2.8 0.0 copy-done.6
  2.8 0.0 copy-done.7
  2.8 0.0 copy-done.8
  2.8 0.0 copy-done.9
  2.9 0.0 copy-done.10
  2.9 49.2 %encode.1 = bf16[4,4,4992]{2,1,0:T(4,128)(2,1)S(1)} custom-call(bf16[4,8,11136]{2,1,0:T(8,128)(2,1)S(1)} %pad.4.feat, bf16[27,96,96]{2,1,0:T(8,128)(2,1)S(1)} %bitcast.12, bf16[27,96,96]{2,1,0:T(8,128)(2,1)S(1)} %bitcast.13, bf16[9,96,96]{2,1,0:T(8,128)(2,1)S(1)} %bitcast.15, f32[1,96]{1,0:T(1,128)S(1)} %bitcast.16, f32[1,96]{1,0:T(1,128)S(1)} %bitcast.17, ...), custom_call_target="tpu_custom_call" | custom-call | tf_op jit(solution)/shard_map/encode/pallas_call | solution.py:509
  52.1 0.7 %copy.16 = bf16[4,4,1,4992]{3,1,2,0:T(4,128)(2,1)} copy(bf16[4,4,1,4992]{3,1,2,0:T(4,128)(2,1)S(1)} %bitcast.14) | data formatting | bytes 319488
Async XLA Ops:
  1.3 0.9 %copy-start.2 = (bf16[3,3,96,96]{3,2,1,0:T(8,128)(2,1)S(1)}, bf16[3,3,96,96]{3,2,1,0:T(8,128)(2,1)}, u32[]{:S(2)}) copy-start(bf16[3,3,96,96]{3,2,1,0:T(8,128)(2,1)} %param.22) | copy-start | bytes 497668
  1.5 1.1 %copy-start = (bf16[3,3,3,96,96]{4,3,2,1,0:T(8,128)(2,1)S(1)}, bf16[3,3,3,96,96]{4,3,2,1,0:T(8,128)(2,1)}, u32[]{:S(2)}) copy-start(bf16[3,3,3,96,96]{4,3,2,1,0:T(8,128)(2,1)} %param.17) | copy-start | bytes 1492996
  1.5 1.3 %copy-start.1 = (bf16[3,3,3,96,96]{4,3,2,1,0:T(8,128)(2,1)S(1)}, bf16[3,3,3,96,96]{4,3,2,1,0:T(8,128)(2,1)}, u32[]{:S(2)}) copy-start(bf16[3,3,3,96,96]{4,3,2,1,0:T(8,128)(2,1)} %param.20) | copy-start | bytes 1492996
  1.5 1.3 %copy-start.3 = (f32[96]{0:T(128)S(1)}, f32[96]{0:T(128)}, u32[]{:S(2)}) copy-start(f32[96]{0:T(128)} %param.16) | copy-start | bytes 1156
  1.5 1.3 %copy-start.4 = (f32[96]{0:T(128)S(1)}, f32[96]{0:T(128)}, u32[]{:S(2)}) copy-start(f32[96]{0:T(128)} %param.18) | copy-start | bytes 1156
  1.5 1.3 %copy-start.5 = (f32[96]{0:T(128)S(1)}, f32[96]{0:T(128)}, u32[]{:S(2)}) copy-start(f32[96]{0:T(128)} %param.19) | copy-start | bytes 1156
  1.6 1.3 %copy-start.6 = (f32[96]{0:T(128)S(1)}, f32[96]{0:T(128)}, u32[]{:S(2)}) copy-start(f32[96]{0:T(128)} %param.21) | copy-start | bytes 1156
  1.6 1.3 %copy-start.7 = (f32[96]{0:T(128)S(1)}, f32[96]{0:T(128)}, u32[]{:S(2)}) copy-start(f32[96]{0:T(128)} %param.23) | copy-start | bytes 1156
  1.6 1.3 %copy-start.8 = (s32[8]{0:T(128)S(1)}, s32[8]{0:T(128)}, u32[]{:S(2)}) copy-start(s32[8]{0:T(128)} %lenh.1) | copy-start | bytes 100
  1.6 1.3 %copy-start.9 = (s32[8]{0:T(128)S(1)}, s32[8]{0:T(128)}, u32[]{:S(2)}) copy-start(s32[8]{0:T(128)} %stoh.1) | copy-start | bytes 100
  1.6 1.3 %copy-start.10 = (s32[8]{0:T(128)S(1)}, s32[8]{0:T(128)}, u32[]{:S(2)}) copy-start(s32[8]{0:T(128)} %ownh.1) | copy-start | bytes 100

commit v4 on v3

--- a/solution.py
+++ b/solution.py
@@ -17,8 +17,6 @@
 OWN = 26
 GROUPS = 9
 WIN = GROUPS * 4
-PADL = 384
-PADR = 768
 LANES = 128
 PAIRS1 = 15
 PAIRS2 = 14
@@ -67,6 +65,10 @@
 
 
 INNER = ((1, 6),)
+AROUND = sorted(
+    ((dx, dy) for dx in range(4) for dy in range(4) if dx or dy),
+    key=lambda d: -(min(d[0], 4 - d[0]) + min(d[1], 4 - d[1])),
+)
 EDGES = ((0, 1), (7, 1))
 EDGES2 = ((0, 1), (7, 2))
 
@@ -90,9 +92,12 @@
         return t, (t // YB, z * YB + t % YB, core)
 
     def start_lane(q):
-        return pl.multiple_of(PADL + CH * (OWN * q - 4 + 2 * (q % 2)), 128)
-
-    arr[:, :, 0:128] = jnp.zeros((16, 8, 128), BF16)
+        return 2304 * q + 128 * (q // 2 - q // 3)
+
+    def place(q):
+        return 384 * (1 - (q + 3) // 4) + 128 * (q // 2 - q // 3)
+
+    arr[:, :, 0:384] = jnp.zeros((16, 8, 384), BF16)
     arr[:, :, 3072:3456] = jnp.zeros((16, 8, 384), BF16)
     barrier = pltpu.get_barrier_semaphore()
 
@@ -133,32 +138,34 @@
     pl.semaphore_wait(barrier, 18)
 
     HALF = 1024
-    odd = y % 2
-
-    def in_copy(i, chunk):
-        t, dev = plane(i)
-        q = t % YB
-        off = 128 * (1 - q % 2) + HALF * chunk
-        src = feat.at[t // YB, :, pl.ds(pl.multiple_of(start_lane(q) + off, 128), HALF)]
-        dst = arr.at[me, :, pl.ds(pl.multiple_of(off, 128), HALF)]
+
+    starts = [start_lane(v) for v in ys_of]
+    offs = [place(v) for v in ys_of]
+
+    def in_copy(dx, dy, chunk):
+        src = feat.at[xs_of[dx], :, pl.ds(pl.multiple_of(starts[dy] + HALF * chunk, 128), HALF)]
+        dst = arr.at[me, :, pl.ds(pl.multiple_of(offs[dy] + HALF * chunk, 128), HALF)]
         return pltpu.make_async_remote_copy(
-            src_ref=src, dst_ref=dst, send_sem=s_a.at[chunk, t], recv_sem=r_a.at[chunk, me],
-            device_id=dev, device_id_type=MESH,
-        )
-
-    my_off = 128 * (1 - odd)
+            src_ref=src, dst_ref=dst,
+            send_sem=s_a.at[chunk, 4 * dx + dy],
+            recv_sem=r_a.at[chunk, 4 * ((4 - dx) % 4) + (4 - dy) % 4],
+            device_id=(xs_of[dx], z * YB + ys_of[dy], core), device_id_type=MESH,
+        )
+
+    my_off = place(y)
     own_in = pltpu.make_async_copy(
-        feat.at[x, :, pl.ds(pl.multiple_of(start_lane(y) + my_off, 128), 3 * HALF)],
+        feat.at[x, :, pl.ds(pl.multiple_of(start_lane(y), 128), 3 * HALF)],
         arr.at[me, :, pl.ds(pl.multiple_of(my_off, 128), 3 * HALF)],
         l_a.at[0],
     )
     own_in.start()
 
-    def start_in(i, _):
-        in_copy(i % 15 + 1, i // 15).start()
-        return 0
-
-    lax.fori_loop(0, 45, start_in, 0)
+    def start_in(chunk, _):
+        for dx, dy in AROUND:
+            in_copy(dx, dy, chunk).start()
+        return 0
+
+    lax.fori_loop(0, 3, start_in, 0)
 
     for c in loads[1:]:
         c.wait()
@@ -180,17 +187,14 @@
     own_in.wait()
 
     def wait_in(chunk):
-        def step(i, _):
-            t, dev = plane(i)
+        for dx, dy in AROUND:
+            t = YB * xs_of[dx] + ys_of[dy]
             dst = arr.at[t, :, pl.ds(pl.multiple_of(my_off + HALF * chunk, 128), HALF)]
             pltpu.make_async_remote_copy(
                 src_ref=feat.at[0, :, pl.ds(0, HALF)], dst_ref=dst,
-                send_sem=s_a.at[chunk, t], recv_sem=r_a.at[chunk, t],
-                device_id=dev, device_id_type=MESH,
+                send_sem=s_a.at[chunk, 4 * dx + dy], recv_sem=r_a.at[chunk, 4 * dx + dy],
+                device_id=(xs_of[dx], z * YB + ys_of[dy], core), device_id_type=MESH,
             ).wait_recv()
-            return 0
-
-        lax.fori_loop(1, 16, step, 0)
 
     lane = lax.broadcasted_iota(jnp.int32, (8, LANES), 1)
     sub8 = lax.broadcasted_iota(jnp.int32, (8, LANES), 0)
@@ -257,7 +261,7 @@
 
         lax.fori_loop(0, count // unit, step, 0)
 
-    base = 2 * (1 - odd)
+    base = 2 * (1 - y % 2) + 4 * (y // 3)
     col0 = OWN * y
 
     def conv1(p0, pairs, rows):
@@ -487,13 +491,12 @@
 
     lax.fori_loop(0, XB, select, 0)
 
-    def end_in(i, _):
-        for chunk in range(3):
-            in_copy(i, chunk).wait_send()
-        return 0
-
-    lax.fori_loop(1, 16, end_in, 0)
-
+    def end_in(chunk, _):
+        for dx, dy in AROUND:
+            in_copy(dx, dy, chunk).wait_send()
+        return 0
+
+    lax.fori_loop(0, 3, end_in, 0)
     lax.fori_loop(0, 8, end_out, 0)
 
 
@@ -503,7 +506,6 @@
 ):
     slots, frames, rows, lanes = features.shape
     feat = jnp.transpose(features, (0, 2, 1, 3)).reshape(slots, rows * frames, lanes)
-    feat = jnp.pad(feat, ((0, 0), (0, 0), (PADL, PADR)))
     hbm = pl.BlockSpec(memory_space=pltpu.HBM)
     dma = pltpu.SemaphoreType.DMA
     result = pl.pallas_call(
@@ -543,7 +545,7 @@
             dma((11,)),
         ],
         compiler_params=pltpu.CompilerParams(
-            collective_id=0, has_side_effects=True, vmem_limit_bytes=50 << 20
+            collective_id=0, has_side_effects=True, vmem_limit_bytes=52 << 20
         ),
         name="encode",
     )(

time: 52.9 us -> 50.9 us (0.962)
  Pallas kernels: 49.2 us -> 47.6 us
    pallas_call x1, Pallas kernels: 49.2 us -> 47.6 us  [local(): pl.pallas_call(kernel, out_shape=jax.ShapeDtypeStruct((slots, frames, 499...]
    unnamed x23 -> x21, local copies, waits for them, and re-layouts: 1.87 us -> 1.59 us
where the time goes in v4:
time: 50.9 us; the launch traced here: 50.8 us
  Pallas kernels  47.6 us (94%)
  local copies, waits for them, and re-layouts  3.06 us (6%)
    pallas_call x1, Pallas kernels, local(): pl.pallas_call(kernel, out_shape=jax.ShapeDtypeStruct((slots, frames, 499...  47.6 us
    unnamed x21, local copies, waits for them, and re-layouts  1.59 us
    transpose x1, local copies, waits for them, and re-layouts, local(): jnp.transpose(features, (0, 2, 1, 3)).reshape(slots, rows * frames, lanes)  1.33 us

profile of v4, /device:TPU:1, one launch (start us, length us, event | category | flops | bytes accessed | tf_op | source)
XLA Modules:
  0.0 50.8 jit_solution(8811187908466729861)
XLA Ops:
  0.0 1.3 %copy.13 = bf16[4,2,4,9984]{3,2,1,0:T(4,128)(2,1)S(1)} copy(bf16[4,2,4,9984]{3,1,2,0:T(2,128)(2,1)} %bitcast.21) | data formatting | bytes 1277952 | tf_op jit(solution)/shard_map/transpose | solution.py:508
  1.3 0.0 copy-start
  1.3 0.0 copy-start.1
  1.4 0.0 copy-start.2
  1.4 0.0 copy-start.3
  1.4 0.0 copy-start.4
  1.4 0.0 copy-start.5
  1.4 0.0 copy-start.6
  1.4 0.0 copy-start.7
  1.4 0.0 copy-start.8
  1.4 0.0 copy-start.9
  1.5 0.1 reshape.30.feat
  1.6 0.8 %copy-done = bf16[3,3,3,96,96]{4,3,2,1,0:T(8,128)(2,1)S(1)} copy-done((bf16[3,3,3,96,96]{4,3,2,1,0:T(8,128)(2,1)S(1)}, bf16[3,3,3,96,96]{4,3,2,1,0:T(8,128)(2,1)}, u32[]{:S(2)}) %copy-start) | copy-done | bytes 497688
  2.4 0.0 copy-done.1
  2.5 0.0 copy-done.2
  2.5 0.0 copy-done.3
  2.5 0.0 copy-done.4
  2.5 0.0 copy-done.5
  2.5 0.0 copy-done.6
  2.5 0.0 copy-done.7
  2.5 0.0 copy-done.8
  2.5 0.0 copy-done.9
  2.5 47.6 %encode.1 = bf16[4,4,4992]{2,1,0:T(4,128)(2,1)S(1)} custom-call(bf16[4,8,9984]{2,1,0:T(8,128)(2,1)S(1)} %reshape.30.feat, bf16[27,96,96]{2,1,0:T(8,128)(2,1)S(1)} %bitcast.12, bf16[27,96,96]{2,1,0:T(8,128)(2,1)} %bitcast.20, bf16[9,96,96]{2,1,0:T(8,128)(2,1)S(1)} %bitcast.14, f32[1,96]{1,0:T(1,128)S(1)} %bitcast.15, f32[1,96]{1,0:T(1,128)S(1)} %bitcast.16, ...), custom_call_target="tpu_custom_call" | custom-call | tf_op jit(solution)/shard_map/encode/pallas_call | solution.py:511
  50.1 0.7 %copy.16 = bf16[4,4,1,4992]{3,1,2,0:T(4,128)(2,1)} copy(bf16[4,4,1,4992]{3,1,2,0:T(4,128)(2,1)S(1)} %bitcast.13) | data formatting | bytes 319488
Async XLA Ops:
  1.3 1.1 %copy-start = (bf16[3,3,3,96,96]{4,3,2,1,0:T(8,128)(2,1)S(1)}, bf16[3,3,3,96,96]{4,3,2,1,0:T(8,128)(2,1)}, u32[]{:S(2)}) copy-start(bf16[3,3,3,96,96]{4,3,2,1,0:T(8,128)(2,1)} %param.17) | copy-start | bytes 1492996
  1.3 1.1 %copy-start.1 = (bf16[3,3,96,96]{3,2,1,0:T(8,128)(2,1)S(1)}, bf16[3,3,96,96]{3,2,1,0:T(8,128)(2,1)}, u32[]{:S(2)}) copy-start(bf16[3,3,96,96]{3,2,1,0:T(8,128)(2,1)} %param.22) | copy-start | bytes 497668
  1.4 1.1 %copy-start.2 = (f32[96]{0:T(128)S(1)}, f32[96]{0:T(128)}, u32[]{:S(2)}) copy-start(f32[96]{0:T(128)} %param.16) | copy-start | bytes 1156
  1.4 1.1 %copy-start.3 = (f32[96]{0:T(128)S(1)}, f32[96]{0:T(128)}, u32[]{:S(2)}) copy-start(f32[96]{0:T(128)} %param.18) | copy-start | bytes 1156
  1.4 1.1 %copy-start.4 = (f32[96]{0:T(128)S(1)}, f32[96]{0:T(128)}, u32[]{:S(2)}) copy-start(f32[96]{0:T(128)} %param.19) | copy-start | bytes 1156
  1.4 1.1 %copy-start.5 = (f32[96]{0:T(128)S(1)}, f32[96]{0:T(128)}, u32[]{:S(2)}) copy-start(f32[96]{0:T(128)} %param.21) | copy-start | bytes 1156
  1.4 1.1 %copy-start.6 = (f32[96]{0:T(128)S(1)}, f32[96]{0:T(128)}, u32[]{:S(2)}) copy-start(f32[96]{0:T(128)} %param.23) | copy-start | bytes 1156
  1.4 1.1 %copy-start.7 = (s32[8]{0:T(128)S(1)}, s32[8]{0:T(128)}, u32[]{:S(2)}) copy-start(s32[8]{0:T(128)} %lenh.1) | copy-start | bytes 100
  1.4 1.1 %copy-start.8 = (s32[8]{0:T(128)S(1)}, s32[8]{0:T(128)}, u32[]{:S(2)}) copy-start(s32[8]{0:T(128)} %stoh.1) | copy-start | bytes 100
  1.4 1.1 %copy-start.9 = (s32[8]{0:T(128)S(1)}, s32[8]{0:T(128)}, u32[]{:S(2)}) copy-start(s32[8]{0:T(128)} %ownh.1) | copy-start | bytes 100

commit v5 on v4

--- a/solution.py
+++ b/solution.py
@@ -65,6 +65,7 @@
 
 
 INNER = ((1, 6),)
+ORDER = (4, 5, 2, 6, 3, 7, 1, 0)
 AROUND = sorted(
     ((dx, dy) for dx in range(4) for dy in range(4) if dx or dy),
     key=lambda d: -(min(d[0], 4 - d[0]) + min(d[1], 4 - d[1])),
@@ -349,12 +350,12 @@
     early_b = z_copy(b.at[2, :, 2], hb.at[2], 33, up)
     early_b.start()
 
-    def end_a(g, _):
-        for c in a_copies(g):
-            c.wait()
-        return 0
-
-    lax.fori_loop(0, GROUPS, end_a, 0)
+    def got_a(g, _):
+        for c in a_copies(g)[:2]:
+            c.wait_recv()
+        return 0
+
+    lax.fori_loop(0, GROUPS, got_a, 0)
     fill_halo(ha, a, WIN, 4, (0, 9))
 
     def b_copies(e):
@@ -400,45 +401,43 @@
     slot = XB * core + x
 
     def out_copy(i, k):
-        xb = (x + k // 2) % XB
-        c = (core + k) % 2
+        xb = xs_of[ORDER[k] // 2]
+        c = core if ORDER[k] % 2 == 0 else 1 - core
         return pltpu.make_async_remote_copy(
             src_ref=sb.at[xb, i], dst_ref=gb.at[slot, y], send_sem=s_g.at[i, k], recv_sem=r_g.at[slot, y],
             device_id=(xb, z * YB + i, c), device_id_type=MESH,
         )
 
-    def end_out(k, _):
-        for i in range(4):
-
-            @pl.when(jnp.logical_not(jnp.logical_and(k == 0, y == i)))
-            def _():
-                out_copy(i, k).wait_send()
-
-        return 0
+    def each_out(i, act):
+        for k in range(8):
+            if ORDER[k]:
+                act(out_copy(i, k))
+            else:
+
+                @pl.when(y != i)
+                def _():
+                    act(out_copy(i, k))
 
     def start_out(i):
-        def step(k, _):
-            here = jnp.logical_and(k == 0, y == i)
-
-            @pl.when(jnp.logical_not(here))
-            def _():
-                out_copy(i, k).start()
-
-            return 0
-
-        lax.fori_loop(0, 8, step, 0)
+        each_out(i, lambda c: c.start())
 
     reduce_rows((1, 2))
     start_out(1)
     start_out(2)
-    early_b.wait()
-
-    def end_b(e, _):
+    early_b.wait_recv()
+
+    def got_b(e, _):
         for c in b_copies(e):
-            c.wait()
-        return 0
-
-    lax.fori_loop(0, 3, end_b, 0)
+            c.wait_recv()
+        return 0
+
+    lax.fori_loop(0, 3, got_b, 0)
+
+    def got_x(g, _):
+        a_copies(g)[2].wait_recv()
+        return 0
+
+    lax.fori_loop(0, GROUPS, got_x, 0)
     fill_halo(hb, b, BC, 5, (0, 9, 10))
 
     def edge2(i, _):
@@ -465,6 +464,29 @@
 
         return 0
 
+    def end_in(chunk, _):
+        for dx, dy in AROUND:
+            in_copy(dx, dy, chunk).wait_send()
+        return 0
+
+    lax.fori_loop(0, 3, end_in, 0)
+    for i in range(4):
+        each_out(i, lambda c: c.wait_send())
+
+    def end_rows(g, _):
+        for c in a_copies(g):
+            c.wait_send()
+        return 0
+
+    lax.fori_loop(0, GROUPS, end_rows, 0)
+
+    def end_b(e, _):
+        for c in b_copies(e):
+            c.wait_send()
+        return 0
+
+    lax.fori_loop(0, 3, end_b, 0)
+    early_b.wait_send()
     lax.fori_loop(0, 32, wait_out, 0)
 
     def select(s, _):
@@ -490,14 +512,6 @@
         return 0
 
     lax.fori_loop(0, XB, select, 0)
-
-    def end_in(chunk, _):
-        for dx, dy in AROUND:
-            in_copy(dx, dy, chunk).wait_send()
-        return 0
-
-    lax.fori_loop(0, 3, end_in, 0)
-    lax.fori_loop(0, 8, end_out, 0)
 
 
 def local(

time: 50.9 us -> 50.7 us (level)
  no operation moved by 1% of the time
where the time goes in v5:
time: 50.7 us; the launch traced here: 50.6 us
  Pallas kernels  47.4 us (93%)
  local copies, waits for them, and re-layouts  3.06 us (6%)
    pallas_call x1, Pallas kernels, local(): pl.pallas_call(kernel, out_shape=jax.ShapeDtypeStruct((slots, frames, 499...  47.4 us
    unnamed x21, local copies, waits for them, and re-layouts  1.59 us
    transpose x1, local copies, waits for them, and re-layouts, local(): jnp.transpose(features, (0, 2, 1, 3)).reshape(slots, rows * frames, lanes)  1.33 us

profile of v5, /device:TPU:1, one launch (start us, length us, event | category | flops | bytes accessed | tf_op | source)
XLA Modules:
  0.0 50.6 jit_solution(1532268456225694695)
XLA Ops:
  0.0 1.3 %copy.13 = bf16[4,2,4,9984]{3,2,1,0:T(4,128)(2,1)S(1)} copy(bf16[4,2,4,9984]{3,1,2,0:T(2,128)(2,1)} %bitcast.21) | data formatting | bytes 1277952 | tf_op jit(solution)/shard_map/transpose | solution.py:522
  1.3 0.0 copy-start
  1.3 0.0 copy-start.1
  1.4 0.0 copy-start.2
  1.4 0.0 copy-start.3
  1.4 0.0 copy-start.4
  1.4 0.0 copy-start.5
  1.4 0.0 copy-start.6
  1.4 0.0 copy-start.7
  1.4 0.0 copy-start.8
  1.4 0.0 copy-start.9
  1.5 0.1 reshape.30.feat
  1.6 0.8 %copy-done = bf16[3,3,3,96,96]{4,3,2,1,0:T(8,128)(2,1)S(1)} copy-done((bf16[3,3,3,96,96]{4,3,2,1,0:T(8,128)(2,1)S(1)}, bf16[3,3,3,96,96]{4,3,2,1,0:T(8,128)(2,1)}, u32[]{:S(2)}) %copy-start) | copy-done | bytes 497688
  2.4 0.0 copy-done.1
  2.5 0.0 copy-done.2
  2.5 0.0 copy-done.3
  2.5 0.0 copy-done.4
  2.5 0.0 copy-done.5
  2.5 0.0 copy-done.6
  2.5 0.0 copy-done.7
  2.5 0.0 copy-done.8
  2.5 0.0 copy-done.9
  2.5 47.4 %encode.1 = bf16[4,4,4992]{2,1,0:T(4,128)(2,1)S(1)} custom-call(bf16[4,8,9984]{2,1,0:T(8,128)(2,1)S(1)} %reshape.30.feat, bf16[27,96,96]{2,1,0:T(8,128)(2,1)S(1)} %bitcast.12, bf16[27,96,96]{2,1,0:T(8,128)(2,1)} %bitcast.20, bf16[9,96,96]{2,1,0:T(8,128)(2,1)S(1)} %bitcast.14, f32[1,96]{1,0:T(1,128)S(1)} %bitcast.15, f32[1,96]{1,0:T(1,128)S(1)} %bitcast.16, ...), custom_call_target="tpu_custom_call" | custom-call | tf_op jit(solution)/shard_map/encode/pallas_call | solution.py:525
  49.9 0.7 %copy.16 = bf16[4,4,1,4992]{3,1,2,0:T(4,128)(2,1)} copy(bf16[4,4,1,4992]{3,1,2,0:T(4,128)(2,1)S(1)} %bitcast.13) | data formatting | bytes 319488
Async XLA Ops:
  1.3 1.1 %copy-start = (bf16[3,3,3,96,96]{4,3,2,1,0:T(8,128)(2,1)S(1)}, bf16[3,3,3,96,96]{4,3,2,1,0:T(8,128)(2,1)}, u32[]{:S(2)}) copy-start(bf16[3,3,3,96,96]{4,3,2,1,0:T(8,128)(2,1)} %param.17) | copy-start | bytes 1492996
  1.3 1.1 %copy-start.1 = (bf16[3,3,96,96]{3,2,1,0:T(8,128)(2,1)S(1)}, bf16[3,3,96,96]{3,2,1,0:T(8,128)(2,1)}, u32[]{:S(2)}) copy-start(bf16[3,3,96,96]{3,2,1,0:T(8,128)(2,1)} %param.22) | copy-start | bytes 497668
  1.4 1.1 %copy-start.2 = (f32[96]{0:T(128)S(1)}, f32[96]{0:T(128)}, u32[]{:S(2)}) copy-start(f32[96]{0:T(128)} %param.16) | copy-start | bytes 1156
  1.4 1.1 %copy-start.3 = (f32[96]{0:T(128)S(1)}, f32[96]{0:T(128)}, u32[]{:S(2)}) copy-start(f32[96]{0:T(128)} %param.18) | copy-start | bytes 1156
  1.4 1.1 %copy-start.4 = (f32[96]{0:T(128)S(1)}, f32[96]{0:T(128)}, u32[]{:S(2)}) copy-start(f32[96]{0:T(128)} %param.19) | copy-start | bytes 1156
  1.4 1.1 %copy-start.5 = (f32[96]{0:T(128)S(1)}, f32[96]{0:T(128)}, u32[]{:S(2)}) copy-start(f32[96]{0:T(128)} %param.21) | copy-start | bytes 1156
  1.4 1.1 %copy-start.6 = (f32[96]{0:T(128)S(1)}, f32[96]{0:T(128)}, u32[]{:S(2)}) copy-start(f32[96]{0:T(128)} %param.23) | copy-start | bytes 1156
  1.4 1.1 %copy-start.7 = (s32[8]{0:T(128)S(1)}, s32[8]{0:T(128)}, u32[]{:S(2)}) copy-start(s32[8]{0:T(128)} %lenh.1) | copy-start | bytes 100
  1.4 1.1 %copy-start.8 = (s32[8]{0:T(128)S(1)}, s32[8]{0:T(128)}, u32[]{:S(2)}) copy-start(s32[8]{0:T(128)} %stoh.1) | copy-start | bytes 100
  1.4 1.1 %copy-start.9 = (s32[8]{0:T(128)S(1)}, s32[8]{0:T(128)}, u32[]{:S(2)}) copy-start(s32[8]{0:T(128)} %ownh.1) | copy-start | bytes 100

commit v6 on v5

--- a/solution.py
+++ b/solution.py
@@ -328,20 +328,16 @@
             z_copy(xs.at[part, 0], xs.at[part, 8], 18 + g, up),
         )
 
-    def outer_rows(g, _):
-        act_step(g, (0, 3))
+    def all_rows(g, _):
+        act_step(g, (0, 1, 2, 3))
         for c in a_copies(g):
             c.start()
         return 0
-
-    def inner_rows(g, _):
-        return act_step(g, (1, 2))
 
     def chunk_step(chunk, _):
         wait_in(chunk)
         g0, g1 = chunk * (chunk + 3) // 2, (chunk + 1) * (chunk + 4) // 2
-        lax.fori_loop(g0, g1, outer_rows, 0)
-        lax.fori_loop(g0, g1, inner_rows, 0)
+        lax.fori_loop(g0, g1, all_rows, 0)
         p0 = jnp.maximum(chunk - 1, 0)
         lax.fori_loop(p0 * (p0 + 3) // 2, chunk * (chunk + 3) // 2, inner1, 0)
         return 0
@@ -559,7 +555,7 @@
             dma((11,)),
         ],
         compiler_params=pltpu.CompilerParams(
-            collective_id=0, has_side_effects=True, vmem_limit_bytes=52 << 20
+            collective_id=0, has_side_effects=True, vmem_limit_bytes=105 << 19
         ),
         name="encode",
     )(

time: 50.7 us -> 49.5 us (0.976)
  Pallas kernels: 47.4 us -> 46.4 us
    pallas_call x1, Pallas kernels: 47.4 us -> 46.4 us  [local(): pl.pallas_call(kernel, out_shape=jax.ShapeDtypeStruct((slots, frames, 499...]
    unnamed x21 -> x19, local copies, waits for them, and re-layouts: 1.59 us -> 1.4 us
where the time goes in v6:
time: 49.5 us; the launch traced here: 49.4 us
  Pallas kernels  46.4 us (94%)
  local copies, waits for them, and re-layouts  2.87 us (6%)
    pallas_call x1, Pallas kernels, local(): pl.pallas_call(kernel, out_shape=jax.ShapeDtypeStruct((slots, frames, 499...  46.4 us
    unnamed x19, local copies, waits for them, and re-layouts  1.4 us
    transpose x1, local copies, waits for them, and re-layouts, local(): jnp.transpose(features, (0, 2, 1, 3)).reshape(slots, rows * frames, lanes)  1.33 us

profile of v6, /device:TPU:1, one launch (start us, length us, event | category | flops | bytes accessed | tf_op | source)
XLA Modules:
  0.0 49.4 jit_solution(9594376780988001189)
XLA Ops:
  0.0 1.3 %copy.13 = bf16[4,2,4,9984]{3,2,1,0:T(4,128)(2,1)S(1)} copy(bf16[4,2,4,9984]{3,1,2,0:T(2,128)(2,1)} %bitcast.21) | data formatting | bytes 1277952 | tf_op jit(solution)/shard_map/transpose | solution.py:518
  1.3 0.0 copy-start
  1.3 0.0 copy-start.1
  1.4 0.0 copy-start.2
  1.4 0.0 copy-start.3
  1.4 0.0 copy-start.4
  1.4 0.0 copy-start.5
  1.4 0.0 copy-start.6
  1.4 0.0 copy-start.7
  1.4 0.0 copy-start.8
  1.4 0.1 reshape.30.feat
  1.6 0.7 %copy-done = bf16[3,3,96,96]{3,2,1,0:T(8,128)(2,1)S(1)} copy-done((bf16[3,3,96,96]{3,2,1,0:T(8,128)(2,1)S(1)}, bf16[3,3,96,96]{3,2,1,0:T(8,128)(2,1)}, u32[]{:S(2)}) %copy-start) | copy-done | bytes 165912
  2.3 0.0 copy-done.1
  2.3 0.0 copy-done.2
  2.3 0.0 copy-done.3
  2.3 0.0 copy-done.4
  2.3 0.0 copy-done.5
  2.3 0.0 copy-done.6
  2.3 0.0 copy-done.7
  2.3 0.0 copy-done.8
  2.3 46.4 %encode.1 = bf16[4,4,4992]{2,1,0:T(4,128)(2,1)S(1)} custom-call(bf16[4,8,9984]{2,1,0:T(8,128)(2,1)S(1)} %reshape.30.feat, bf16[27,96,96]{2,1,0:T(8,128)(2,1)} %bitcast.19, bf16[27,96,96]{2,1,0:T(8,128)(2,1)} %bitcast.20, bf16[9,96,96]{2,1,0:T(8,128)(2,1)S(1)} %bitcast.13, f32[1,96]{1,0:T(1,128)S(1)} %bitcast.14, f32[1,96]{1,0:T(1,128)S(1)} %bitcast.15, ...), custom_call_target="tpu_custom_call" | custom-call | tf_op jit(solution)/shard_map/encode/pallas_call | solution.py:521
  48.7 0.7 %copy.16 = bf16[4,4,1,4992]{3,1,2,0:T(4,128)(2,1)} copy(bf16[4,4,1,4992]{3,1,2,0:T(4,128)(2,1)S(1)} %bitcast.12) | data formatting | bytes 319488
Async XLA Ops:
  1.3 0.9 %copy-start = (bf16[3,3,96,96]{3,2,1,0:T(8,128)(2,1)S(1)}, bf16[3,3,96,96]{3,2,1,0:T(8,128)(2,1)}, u32[]{:S(2)}) copy-start(bf16[3,3,96,96]{3,2,1,0:T(8,128)(2,1)} %param.22) | copy-start | bytes 497668
  1.3 0.9 %copy-start.1 = (f32[96]{0:T(128)S(1)}, f32[96]{0:T(128)}, u32[]{:S(2)}) copy-start(f32[96]{0:T(128)} %param.16) | copy-start | bytes 1156
  1.4 0.9 %copy-start.2 = (f32[96]{0:T(128)S(1)}, f32[96]{0:T(128)}, u32[]{:S(2)}) copy-start(f32[96]{0:T(128)} %param.18) | copy-start | bytes 1156
  1.4 0.9 %copy-start.3 = (f32[96]{0:T(128)S(1)}, f32[96]{0:T(128)}, u32[]{:S(2)}) copy-start(f32[96]{0:T(128)} %param.19) | copy-start | bytes 1156
  1.4 0.9 %copy-start.4 = (f32[96]{0:T(128)S(1)}, f32[96]{0:T(128)}, u32[]{:S(2)}) copy-start(f32[96]{0:T(128)} %param.21) | copy-start | bytes 1156
  1.4 0.9 %copy-start.5 = (f32[96]{0:T(128)S(1)}, f32[96]{0:T(128)}, u32[]{:S(2)}) copy-start(f32[96]{0:T(128)} %param.23) | copy-start | bytes 1156
  1.4 0.9 %copy-start.6 = (s32[8]{0:T(128)S(1)}, s32[8]{0:T(128)}, u32[]{:S(2)}) copy-start(s32[8]{0:T(128)} %lenh.1) | copy-start | bytes 100
  1.4 0.9 %copy-start.7 = (s32[8]{0:T(128)S(1)}, s32[8]{0:T(128)}, u32[]{:S(2)}) copy-start(s32[8]{0:T(128)} %stoh.1) | copy-start | bytes 100
  1.4 0.9 %copy-start.8 = (s32[8]{0:T(128)S(1)}, s32[8]{0:T(128)}, u32[]{:S(2)}) copy-start(s32[8]{0:T(128)} %ownh.1) | copy-start | bytes 100

commit v7 on v6

--- a/solution.py
+++ b/solution.py
@@ -317,7 +317,7 @@
                     at += count
 
     def inner1(i, _):
-        conv1(3 * i, 3, INNER)
+        conv1(5 * i, 5, INNER)
         return 0
 
     def a_copies(g):
@@ -339,7 +339,7 @@
         g0, g1 = chunk * (chunk + 3) // 2, (chunk + 1) * (chunk + 4) // 2
         lax.fori_loop(g0, g1, all_rows, 0)
         p0 = jnp.maximum(chunk - 1, 0)
-        lax.fori_loop(p0 * (p0 + 3) // 2, chunk * (chunk + 3) // 2, inner1, 0)
+        lax.fori_loop(p0 * (p0 + 1) // 2, chunk * (chunk + 1) // 2, inner1, 0)
         return 0
 
     lax.fori_loop(0, 3, chunk_step, 0)

time: 49.5 us -> 48.8 us (0.986)
  Pallas kernels: 46.4 us -> 45.7 us
    pallas_call x1, Pallas kernels: 46.4 us -> 45.7 us  [local(): pl.pallas_call(kernel, out_shape=jax.ShapeDtypeStruct((slots, frames, 499...]
where the time goes in v7:
time: 48.8 us; the launch traced here: 48.7 us
  Pallas kernels  45.7 us (94%)
  local copies, waits for them, and re-layouts  2.87 us (6%)
    pallas_call x1, Pallas kernels, local(): pl.pallas_call(kernel, out_shape=jax.ShapeDtypeStruct((slots, frames, 499...  45.7 us
    unnamed x19, local copies, waits for them, and re-layouts  1.4 us
    transpose x1, local copies, waits for them, and re-layouts, local(): jnp.transpose(features, (0, 2, 1, 3)).reshape(slots, rows * frames, lanes)  1.33 us

profile of v7, /device:TPU:1, one launch (start us, length us, event | category | flops | bytes accessed | tf_op | source)
XLA Modules:
  0.0 48.7 jit_solution(4145688011528452769)
XLA Ops:
  0.0 1.3 %copy.13 = bf16[4,2,4,9984]{3,2,1,0:T(4,128)(2,1)S(1)} copy(bf16[4,2,4,9984]{3,1,2,0:T(2,128)(2,1)} %bitcast.21) | data formatting | bytes 1277952 | tf_op jit(solution)/shard_map/transpose | solution.py:518
  1.3 0.0 copy-start
  1.3 0.0 copy-start.1
  1.4 0.0 copy-start.2
  1.4 0.0 copy-start.3
  1.4 0.0 copy-start.4
  1.4 0.0 copy-start.5
  1.4 0.0 copy-start.6
  1.4 0.0 copy-start.7
  1.4 0.0 copy-start.8
  1.4 0.1 reshape.30.feat
  1.6 0.7 %copy-done = bf16[3,3,96,96]{3,2,1,0:T(8,128)(2,1)S(1)} copy-done((bf16[3,3,96,96]{3,2,1,0:T(8,128)(2,1)S(1)}, bf16[3,3,96,96]{3,2,1,0:T(8,128)(2,1)}, u32[]{:S(2)}) %copy-start) | copy-done | bytes 165912
  2.3 0.0 copy-done.1
  2.3 0.0 copy-done.2
  2.3 0.0 copy-done.3
  2.3 0.0 copy-done.4
  2.3 0.0 copy-done.5
  2.3 0.0 copy-done.6
  2.3 0.0 copy-done.7
  2.3 0.0 copy-done.8
  2.3 45.7 %encode.1 = bf16[4,4,4992]{2,1,0:T(4,128)(2,1)S(1)} custom-call(bf16[4,8,9984]{2,1,0:T(8,128)(2,1)S(1)} %reshape.30.feat, bf16[27,96,96]{2,1,0:T(8,128)(2,1)} %bitcast.19, bf16[27,96,96]{2,1,0:T(8,128)(2,1)} %bitcast.20, bf16[9,96,96]{2,1,0:T(8,128)(2,1)S(1)} %bitcast.13, f32[1,96]{1,0:T(1,128)S(1)} %bitcast.14, f32[1,96]{1,0:T(1,128)S(1)} %bitcast.15, ...), custom_call_target="tpu_custom_call" | custom-call | tf_op jit(solution)/shard_map/encode/pallas_call | solution.py:521
  48.0 0.7 %copy.16 = bf16[4,4,1,4992]{3,1,2,0:T(4,128)(2,1)} copy(bf16[4,4,1,4992]{3,1,2,0:T(4,128)(2,1)S(1)} %bitcast.12) | data formatting | bytes 319488
Async XLA Ops:
  1.3 0.9 %copy-start = (bf16[3,3,96,96]{3,2,1,0:T(8,128)(2,1)S(1)}, bf16[3,3,96,96]{3,2,1,0:T(8,128)(2,1)}, u32[]{:S(2)}) copy-start(bf16[3,3,96,96]{3,2,1,0:T(8,128)(2,1)} %param.22) | copy-start | bytes 497668
  1.3 0.9 %copy-start.1 = (f32[96]{0:T(128)S(1)}, f32[96]{0:T(128)}, u32[]{:S(2)}) copy-start(f32[96]{0:T(128)} %param.16) | copy-start | bytes 1156
  1.4 0.9 %copy-start.2 = (f32[96]{0:T(128)S(1)}, f32[96]{0:T(128)}, u32[]{:S(2)}) copy-start(f32[96]{0:T(128)} %param.18) | copy-start | bytes 1156
  1.4 0.9 %copy-start.3 = (f32[96]{0:T(128)S(1)}, f32[96]{0:T(128)}, u32[]{:S(2)}) copy-start(f32[96]{0:T(128)} %param.19) | copy-start | bytes 1156
  1.4 0.9 %copy-start.4 = (f32[96]{0:T(128)S(1)}, f32[96]{0:T(128)}, u32[]{:S(2)}) copy-start(f32[96]{0:T(128)} %param.21) | copy-start | bytes 1156
  1.4 0.9 %copy-start.5 = (f32[96]{0:T(128)S(1)}, f32[96]{0:T(128)}, u32[]{:S(2)}) copy-start(f32[96]{0:T(128)} %param.23) | copy-start | bytes 1156
  1.4 0.9 %copy-start.6 = (s32[8]{0:T(128)S(1)}, s32[8]{0:T(128)}, u32[]{:S(2)}) copy-start(s32[8]{0:T(128)} %lenh.1) | copy-start | bytes 100
  1.4 0.9 %copy-start.7 = (s32[8]{0:T(128)S(1)}, s32[8]{0:T(128)}, u32[]{:S(2)}) copy-start(s32[8]{0:T(128)} %stoh.1) | copy-start | bytes 100
  1.4 0.9 %copy-start.8 = (s32[8]{0:T(128)S(1)}, s32[8]{0:T(128)}, u32[]{:S(2)}) copy-start(s32[8]{0:T(128)} %ownh.1) | copy-start | bytes 100
